TPU v7x, 128 devices: a whole 4x4x4 slice. The times are simulated.
128 devices in a mesh: list: 8 (over z, core), fsdp: 16 (over x, y).
Axes of the slice: x: 4, y: 4, z: 4, core: 2. Of those that a mesh axis runs over, the one named last changes fastest.
Arguments:
- hidden: bfloat16 [2048, 64, 2048], P(('list', 'fsdp')), may hold values from -6 to 6
- norm_gain: float32 [2048], replicated, may hold values from 0.5 to 1.5
- w_qkv: bfloat16 [2048, 1536], P('fsdp'), may hold values from -0.125 to 0.125
- w_out: bfloat16 [1024, 2048], P('fsdp'), may hold values from -0.1875 to 0.1875
- final_gain: float32 [2048], replicated, may hold values from 0.5 to 1.5
- w_score: float32 [2048], replicated, may hold values from -0.125 to 0.125
- prior: float32 [2048], P(('list', 'fsdp')), may hold values from -8 to 400
- labels: int32 [2048], P(('list', 'fsdp')), may hold values from 0 to 3
- lengths: int32 [64], replicated, may hold values from 1 to 48, 2048 in all
Outputs:
- loss: float32 [], replicated
- grad_qkv: float32 [2048, 1536], P('fsdp', 'list')
- grad_out: float32 [1024, 2048], P('fsdp', 'list')
Inputs may be any that keep to these rules, and one draw needn't show every extreme that they name: `lengths`: the longest list holds exactly 48 passages.
All inputs are finite; a program needn't handle non-finite values.
Results may differ from a plain program's by a relative error of at most 0.025.
Values may be sent and summed in bfloat16 or wider, within the bound.
A program may use at most 128 MiB of HBM per device.

v0:
```python
import jax
import jax.numpy as jnp
from jax import lax
from jax.sharding import Mesh
from jax.sharding import PartitionSpec as P

HEADS = 16
KV_HEADS = 4
HEAD_DIM = 64
PASSAGE_LEN = 64
FSDP = ("fsdp_0", "fsdp_1")
LIST_FSDP = ("list_0", "list_1", "fsdp_0", "fsdp_1")
LIST = ("list_0", "list_1")


epsilon = 1e-05
loss_scale = 64.0


def collected_together(value, axis):
    leaves = jax.tree.leaves(value)
    order = sorted(range(len(leaves)), key=lambda k: -leaves[k].size)
    width = (1, *leaves[order[0]].shape)[-1]
    lines = [
        jnp.pad(leaves[k].reshape(-1), (0, -leaves[k].size % width)).reshape(-1, width)
        for k in order
    ]
    both, at, found = (lax.all_gather(jnp.concatenate(lines), axis), 0, {})
    for k, line in zip(order, lines):
        slab = both[:, at : at + len(line)].reshape(len(both), -1)
        found[k] = slab[:, : leaves[k].size].reshape(-1, *leaves[k].shape)
        at += len(line)
    numbers = iter(range(len(leaves)))
    return jax.tree.map(lambda _: found[next(numbers)], value)


def joined_all(value, axes, combine):
    for axis in axes:
        pieces = collected_together(value, axis)
        value = jax.tree.map(lambda part: part[0], pieces)
        for k in range(1, lax.axis_size(axis)):
            value = combine(value, jax.tree.map(lambda part: part[k], pieces))
    return value


def by_axis(value, axes):
    for axis in axes:
        value = lax.psum(value, axis)
    return value


def own_rows(terms, axes):
    so_far = terms.astype(jnp.bfloat16)
    for axis in axes:
        so_far = lax.psum_scatter(so_far, axis, scatter_dimension=0, tiled=True)
    return so_far.astype(jnp.float32)


def joined_along(parts, dim):
    dims = list(parts.shape[1:])
    dims[dim] *= parts.shape[0]
    return jnp.moveaxis(parts, 0, dim).reshape(dims)


def from_everyone(value, axis):
    copies = jnp.broadcast_to(value, (lax.axis_size(axis), *value.shape))
    return lax.all_to_all(copies, axis, split_axis=0, concat_axis=0, tiled=True)


def gathered_copies(value, axis, dim):
    return joined_along(from_everyone(value, axis), dim)


def in_blocks(value, dim, count):
    dims = value.shape
    parts = value.reshape(*dims[:dim], count, dims[dim] // count, *dims[dim + 1 :])
    return jnp.moveaxis(parts, dim, 0)


def sum_packed(arrays, axis, dims):
    count = lax.axis_size(axis)
    parts = [in_blocks(a, dim, count) for a, dim in zip(arrays, dims)]
    lines = jnp.concatenate([b.reshape(count, -1) for b in parts], axis=1)
    width = max(16, -(-lines.shape[1] // 1024) * 8)
    lines = jnp.pad(lines, ((0, 0), (0, width * 128 - lines.shape[1]))).reshape(-1, 128)
    flat, at, gathered = (lax.psum_scatter(lines, axis, tiled=True).reshape(-1), 0, [])
    for b in parts:
        part = b[0]
        gathered.append(flat[at : at + part.size].reshape(part.shape))
        at += part.size
    return tuple(gathered)


def normed(hidden, norm_gain):
    values = hidden.astype(jnp.float32)
    mean_square = jnp.mean(values * values, -1, keepdims=True)
    return (values * lax.rsqrt(mean_square + epsilon) * norm_gain).astype(jnp.bfloat16)


def attend(projected, passages):
    width_q = HEADS * HEAD_DIM
    width_k = KV_HEADS * HEAD_DIM
    ratio = HEADS // KV_HEADS
    query_part = projected[:, :width_q].reshape(passages, PASSAGE_LEN, KV_HEADS, ratio, HEAD_DIM)
    key_part = projected[:, width_q : width_q + width_k].reshape(
        passages, PASSAGE_LEN, KV_HEADS, HEAD_DIM
    )
    value_part = projected[:, width_q + width_k :].reshape(
        passages, PASSAGE_LEN, KV_HEADS, HEAD_DIM
    )
    scores = jnp.einsum(
        "bqgre,bkge->bgrqk", query_part, key_part, preferred_element_type=jnp.float32
    ) * HEAD_DIM ** (-0.5)
    peak = jnp.max(scores, -1, keepdims=True)
    expo = jnp.exp(scores - peak)
    probs = (expo / jnp.sum(expo, -1, keepdims=True)).astype(jnp.bfloat16)
    attended = jnp.einsum(
        "bgrqk,bkge->bqgre", probs, value_part, preferred_element_type=jnp.float32
    ).astype(jnp.bfloat16)
    return (
        query_part,
        key_part,
        value_part,
        probs,
        attended.reshape(passages, PASSAGE_LEN, width_q),
    )


def attend_back(query_part, key_part, value_part, probs, d_attended, passages):
    d_heads = d_attended.reshape(passages, KV_HEADS, HEADS // KV_HEADS, HEAD_DIM)
    d_probs = jnp.einsum("bgre,bkge->bgrk", d_heads, value_part, preferred_element_type=jnp.float32)
    probs_f = probs.astype(jnp.float32)
    inner = jnp.sum(probs_f * d_probs[:, :, :, None, :], -1, keepdims=True)
    d_scores = (probs_f * (d_probs[:, :, :, None, :] - inner) * HEAD_DIM ** (-0.5)).astype(
        jnp.bfloat16
    )
    d_query = jnp.einsum(
        "bgrqk,bkge->bqgre", d_scores, key_part, preferred_element_type=jnp.float32
    ).astype(jnp.bfloat16)
    d_key = jnp.einsum(
        "bgrqk,bqgre->bkge", d_scores, query_part, preferred_element_type=jnp.float32
    ).astype(jnp.bfloat16)
    d_value = jnp.einsum(
        "bgrqk,bgre->bkge", probs, d_heads, preferred_element_type=jnp.float32
    ).astype(jnp.bfloat16)
    rows = passages * PASSAGE_LEN
    return jnp.concatenate(
        [d_query.reshape(rows, -1), d_key.reshape(rows, -1), d_value.reshape(rows, -1)], 1
    )


def combine_stats(first, second):
    peak = jnp.maximum(first[0], second[0])
    total = first[1] * jnp.exp(first[0] - peak) + second[1] * jnp.exp(second[0] - peak)
    return (peak, total, first[2] + second[2])


def local(hidden, norm_gain, w_qkv, w_out, final_gain, w_score, prior, labels, lengths):
    passages = hidden.shape[0]
    width = hidden.shape[2]
    normal_rows = normed(hidden, norm_gain).reshape(passages * PASSAGE_LEN, width)
    full_qkv, full_out = (
        lax.all_gather(w_qkv, FSDP, axis=0, tiled=True),
        lax.all_gather(w_out, FSDP, axis=0, tiled=True),
    )
    projected = jnp.dot(normal_rows, full_qkv, preferred_element_type=jnp.float32).astype(
        jnp.bfloat16
    )
    query_part, key_part, value_part, probs, attended = attend(projected, passages)
    mixed = jnp.dot(
        attended.reshape(passages * PASSAGE_LEN, -1), full_out, preferred_element_type=jnp.float32
    )
    residual = hidden.astype(jnp.float32) + mixed.reshape(passages, PASSAGE_LEN, width)
    pooled = jnp.mean(residual, 1)
    inverse = lax.rsqrt(jnp.mean(pooled * pooled, -1, keepdims=True) + epsilon)
    unit = pooled * inverse
    score = jnp.sum(unit * final_gain * w_score, -1) + prior
    queries = lengths.shape[0]
    position = lax.axis_index(LIST_FSDP) * passages + jnp.arange(passages, dtype=jnp.int32)
    ends = jnp.cumsum(lengths)
    owner = jnp.sum((position[:, None] >= ends[None, :]).astype(jnp.int32), 1)
    member = (owner[:, None] == jnp.arange(queries, dtype=jnp.int32)[None, :]).astype(jnp.float32)
    label_weight = jnp.exp(labels.astype(jnp.float32))
    label_local = jnp.sum(member * label_weight[:, None], 0)
    local_peak = jnp.max(jnp.where(member > 0, score[:, None], -1e30), 0)
    own_peak = jnp.sum(member * local_peak[None, :], 1)
    expo_local = jnp.sum(member * jnp.exp(score - own_peak)[:, None], 0)
    peak, total, label_total = joined_all(
        (local_peak, expo_local, label_local), LIST_FSDP, combine_stats
    )
    log_norm = peak + jnp.log(total)
    log_prob = score - jnp.sum(member * log_norm[None, :], 1)
    target = label_weight / jnp.sum(member * label_total[None, :], 1)
    loss = by_axis(-loss_scale * jnp.sum(target * log_prob), LIST_FSDP)
    d_score = loss_scale * (jnp.exp(log_prob) - target)
    d_unit = d_score[:, None] * w_score[None, :] * final_gain[None, :]
    d_pooled = inverse * (d_unit - unit * jnp.mean(d_unit * unit, -1, keepdims=True))
    d_rows = (d_pooled / PASSAGE_LEN).astype(jnp.bfloat16)
    attn_sum = jnp.sum(attended, 1, dtype=jnp.float32).astype(jnp.bfloat16)
    d_attended = lax.dot_general(
        d_rows, full_out, (((1,), (1,)), ((), ())), preferred_element_type=jnp.float32
    ).astype(jnp.bfloat16)
    d_projected = attend_back(query_part, key_part, value_part, probs, d_attended, passages)
    qkv_part = own_rows(
        lax.dot_general(
            normal_rows, d_projected, (((0,), (0,)), ((), ())), preferred_element_type=jnp.float32
        ),
        FSDP,
    )
    group_sums = lax.all_to_all(attn_sum, FSDP, split_axis=1, concat_axis=0, tiled=True)
    group_rows = gathered_copies(d_rows, FSDP, 0)
    out_part = lax.dot_general(
        group_sums, group_rows, (((0,), (0,)), ((), ())), preferred_element_type=jnp.float32
    )
    grad_qkv, grad_out = tuple(
        (
            part.astype(jnp.float32)
            for part in sum_packed(
                (qkv_part.astype(jnp.bfloat16), out_part.astype(jnp.bfloat16)), LIST, (1, 1)
            )
        )
    )
    return (loss, grad_qkv, grad_out)


def solution(mesh):
    torus = Mesh(mesh.devices.reshape(4, 2, 4, 4), ("list_0", "list_1", "fsdp_0", "fsdp_1"))
    in_specs = (
        P(LIST_FSDP, None, None),
        P(),
        P(FSDP, None),
        P(FSDP, None),
        P(),
        P(),
        P(LIST_FSDP),
        P(LIST_FSDP),
        P(),
    )
    out_specs = (P(), P(FSDP, LIST), P(FSDP, LIST))
    return jax.shard_map(local, mesh=torus, in_specs=in_specs, out_specs=out_specs, check_vma=False)
```

profile of v0, /device:TPU:0, one launch (start us, length us, event | category | flops | bytes accessed | tf_op | source)
XLA Modules:
  0.0 379.8 jit_solution(12760999220482166367)
XLA Ops:
  7.2 0.7 all-gather.11.cloned.1.call-update
  8.0 0.7 all-gather.13.cloned.1.call-update
  8.7 0.7 copy.57
  9.9 3.2 fusion.3
  13.1 3.0 fusion.5
  16.1 57.7 %all-gather.11.cloned.1.call-done = bf16[2048,1536]{1,0:T(8,128)(2,1)} async-done(((bf16[128,1536]{1,0:T(8,128)(2,1)}), bf16[2048,1536]{1,0:T(8,128)(2,1)}) %all-gather.11.cloned.1.call-update) | async-done | bytes 6291472 | tf_op jit(solution)/shard_map/all_gather | solution.py:163
  73.8 10.0 %convolution_convert_fusion.1 = bf16[1024,1536]{1,0:T(8,128)(2,1)S(1)} fusion(bf16[1024,2048]{1,0:T(8,128)(2,1)} %bitcast.332, bf16[2048,1536]{1,0:T(8,128)(2,1)} %all-gather.11.cloned.1.call-done), kind=kOutput, calls=%fused_computation.28 | convolution fusion | flops 6444023808 | bytes 13631488 | tf_op jit(solution)/shard_map/dot_general | solution.py:166
  84.2 1.1 fusion.91
  85.3 2.0 reshape.843
  87.3 1.4 copy.78
  88.7 4.0 %reshape.844 = bf16[16,64,4,4,64]{4,3,2,1,0:T(4,128)(2,1)} reshape(bf16[1024,1024]{1,0:T(8,128)(2,1)S(1)} %slice.288) | data formatting | bytes 4194304 | tf_op jit(solution)/shard_map/reshape | solution.py:104
  92.7 8.3 %copy.67 = bf16[16,64,4,4,64]{1,4,3,2,0:T(8,128)(2,1)} copy(bf16[16,64,4,4,64]{4,3,2,1,0:T(4,128)(2,1)} %reshape.844) | data formatting | bytes 4194304 | tf_op jit(solution)/shard_map/reshape | solution.py:104
  101.4 8.6 %fusion.92 = (f32[16,4,4,64]{3,2,1,0:T(4,128)S(1)}, f32[16,4,4,64,64]{3,4,2,1,0:T(8,128)}) fusion(bf16[16,64,4,64,1]{1,3,4,2,0:T(8,128)(2,1)S(1)} %copy-done.3, bf16[16,64,4,4,64]{1,4,3,2,0:T(8,128)(2,1)} %copy.67), kind=kOutput, calls=%fused_computation.172 | convolution fusion | flops 137363520 | bytes 6881280 | tf_op jit(solution)/shard_map/sub | solution.py:115
  110.1 5.7 %convert_reduce_fusion = (bf16[16,4,4,64]{3,2,1,0:T(4,128)(2,1)S(1)}, bf16[16,4,4,64,64]{3,4,2,1,0:T(8,128)(2,1)S(1)}) fusion(f32[16,4,4,64,64]{3,4,2,1,0:T(8,128)} %get-tuple-element.31, f32[16,4,4,64]{3,2,1,0:T(4,128)S(1)} %get-tuple-element.30), kind=kLoop, calls=%fused_computation.2 | loop fusion | flops 4177920 | bytes 6389760 | tf_op jit(solution)/shard_map/bgrqk,bgre->bkge/reduce_sum | solution.py:143
  115.8 2.1 fusion.93
  118.0 5.4 %copy.62 = bf16[16,64,4,4,64]{4,3,2,1,0:T(4,128)(2,1)} copy(bf16[16,64,4,4,64]{4,1,3,2,0:T(8,128)(2,1)S(1)} %get-tuple-element.33) | data formatting | bytes 4194304 | tf_op jit(solution)/shard_map/convert_element_type | solution.py:119
  123.4 8.2 %dot_general.38 = bf16[16,64,1024]{2,1,0:T(8,128)(2,1)} reshape(bf16[16,64,4,4,64]{4,3,2,1,0:T(4,128)(2,1)} %copy.62) | data formatting | bytes 4194304 | tf_op jit(solution)/shard_map/dot_general | solution.py:170
  131.6 8.7 %fusion.6 = f32[16,2048]{1,0:T(8,128)S(1)} fusion(bf16[16,64,2048]{2,1,0:T(8,128)(2,1)} %param.9, bf16[16,64,1024]{2,1,0:T(8,128)(2,1)} %dot_general.38, bf16[1024,2048]{1,0:T(8,128)(2,1)} %all-gather.13.cloned.1.call-done), kind=kOutput, calls=%fused_computation.12 | convolution fusion | flops 4301225984 | bytes 10616832 | tf_op jit(solution)/shard_map/dot_general | solution.py:170
  141.1 11.3 %all-gather.4 = f32[4,3,64]{2,1,0:T(4,128)S(1)} all-gather(f32[1,3,64]{2,1,0:T(4,128)S(1)} %maximum_bitcast_fusion), channel_id=2, replica_groups=mesh['list_0'=4,'list_1'=2,'fsdp_0'=4,'fsdp_1'=4] {'list_0'}, dimensions={0}, use_global_device_ids=true | all-gather | bytes 3840 | tf_op jit(solution)/shard_map/all_gather | solution.py:28
  152.5 1.8 all-gather.5
  154.4 11.1 %all-gather.6 = f32[4,3,64]{2,1,0:T(4,128)S(1)} all-gather(f32[1,3,64]{2,1,0:T(4,128)S(1)} %maximum_bitcast_fusion.2), channel_id=4, replica_groups=mesh['list_0'=4,'list_1'=2,'fsdp_0'=4,'fsdp_1'=4] {'fsdp_0'}, dimensions={0}, use_global_device_ids=true | all-gather | bytes 3840 | tf_op jit(solution)/shard_map/all_gather | solution.py:28
  165.5 10.4 %all-gather.7 = f32[4,3,64]{2,1,0:T(4,128)S(1)} all-gather(f32[1,3,64]{2,1,0:T(4,128)S(1)} %maximum_bitcast_fusion.3), channel_id=5, replica_groups=mesh['list_0'=4,'list_1'=2,'fsdp_0'=4,'fsdp_1'=4] {'fsdp_1'}, dimensions={0}, use_global_device_ids=true | all-gather | bytes 3840 | tf_op jit(solution)/shard_map/all_gather | solution.py:28
  176.6 1.2 convolution_convert_fusion.3
  178.5 8.8 %convert_bitcast_fusion = bf16[16,64,4,4,64]{1,4,3,2,0:T(8,128)(2,1)} fusion(bf16[16,64,4,64,1]{1,3,4,2,0:T(8,128)(2,1)S(1)} %copy-done.3, bf16[16,4,4,64,64]{3,4,2,1,0:T(8,128)(2,1)} %copy-done, f32[16,4,4,64]{3,2,1,0:T(4,128)S(1)} %fusion.31), kind=kOutput, calls=%fused_computation.24 | convolution fusion | flops 142622784 | bytes 4784128 | tf_op jit(solution)/shard_map/bgrqk,bkge->bqgre/dot_general | solution.py:137
  187.3 10.4 %fusion.28 = bf16[16,64,4,64]{1,3,2,0:T(8,128)(2,1)} fusion(bf16[16,64,4,4,64]{1,4,3,2,0:T(8,128)(2,1)} %copy.67, bf16[16,4,4,64,64]{3,4,2,1,0:T(8,128)(2,1)} %copy-done, f32[16,4,4,64]{3,2,1,0:T(4,128)S(1)} %fusion.31), kind=kOutput, calls=%fused_computation.40 | convolution fusion | flops 141836352 | bytes 4784128 | tf_op jit(solution)/shard_map/bgrqk,bqgre->bkge/dot_general | solution.py:140
  197.7 7.6 %copy.66 = bf16[16,64,4,4,64]{1,0,4,3,2:T(8,128)(2,1)} copy(bf16[16,64,4,4,64]{1,4,3,2,0:T(8,128)(2,1)} %convert_bitcast_fusion) | data formatting | bytes 4194304 | tf_op jit(solution)/shard_map/convert_element_type | solution.py:139
  205.4 5.5 %reshape.849 = bf16[1024,1024]{0,1:T(8,128)(2,1)S(1)} reshape(bf16[16,64,4,4,64]{1,0,4,3,2:T(8,128)(2,1)} %copy.66) | data formatting | bytes 4194304 | tf_op jit(solution)/shard_map/reshape | solution.py:148
  210.8 1.9 copy.69
  212.7 1.5 reshape.850
  214.8 0.7 copy.70
  215.5 1.5 reshape.851
  217.0 11.8 %convolution_convert_fusion = bf16[2048,1536]{1,0:T(8,128)(2,1)} fusion(bf16[1024,2048]{1,0:T(8,128)(2,1)} %bitcast.333, bf16[1024,256]{0,1:T(8,128)(2,1)} %reshape.851, bf16[1024,256]{0,1:T(8,128)(2,1)} %reshape.850, bf16[1024,1024]{0,1:T(8,128)(2,1)S(1)} %reshape.849), kind=kOutput, calls=%fused_computation.20 | convolution fusion | flops 6455033856 | bytes 13631488 | tf_op jit(solution)/shard_map/dot_general | solution.py:205
  228.8 62.7 %reduce-scatter.4.cloned.1.call-done = bf16[512,1536]{1,0:T(8,128)(2,1)} async-done(((bf16[2048,1536]{1,0:T(8,128)(2,1)}), bf16[512,1536]{1,0:T(8,128)(2,1)}) %reduce-scatter.4.cloned.1.call-update) | async-done | bytes 1572880 | tf_op jit(solution)/shard_map/reduce_scatter | solution.py:55
  291.7 12.7 %all_to_all.21 = bf16[16,2,512]{2,1,0:T(2,128)(2,1)S(1)} all-to-all(bf16[16,2,512]{2,1,0:T(2,128)(2,1)S(1)} %reshape.882), channel_id=1, replica_groups=mesh['list_0'=4,'list_1'=2,'fsdp_0'=4,'fsdp_1'=4] {'fsdp_0','fsdp_1'}, dimensions={0} | all-to-all | bytes 65536 | tf_op jit(solution)/shard_map/all_to_all | solution.py:210
  304.4 1.1 broadcast_in_dim.12
  305.5 3.7 all-to-all-start.1
  309.4 16.2 %all-to-all-done.1 = bf16[16,16,2048]{2,1,0:T(8,128)(2,1)S(1)} async-done(((bf16[16,16,2048]{2,1,0:T(8,128)(2,1)}), bf16[16,16,2048]{2,1,0:T(8,128)(2,1)S(1)}, u32[]{:S(2)}, u32[]{:S(2)}) %all-to-all-start.1) | async-done | bytes 1048608 | tf_op jit(solution)/shard_map/all_to_all | solution.py:67
  326.0 4.3 %reduce-scatter.6.cloned.1.call-done = bf16[128,1536]{1,0:T(8,128)(2,1)} async-done(((bf16[512,1536]{1,0:T(8,128)(2,1)}), bf16[128,1536]{1,0:T(8,128)(2,1)}) %reduce-scatter.6.cloned.1.call-update) | async-done | bytes 393232 | tf_op jit(solution)/shard_map/reduce_scatter | solution.py:55
  330.3 1.2 copy.71
  332.3 1.1 reshape.856
  334.7 11.2 %psum.28 = f32[]{:T(128)} all-reduce(f32[]{:T(128)S(6)} %mul_shard_map.3), channel_id=1, replica_groups=mesh['list_0'=4,'list_1'=2,'fsdp_0'=4,'fsdp_1'=4] {'list_0'}, use_global_device_ids=true, to_apply=%region_15.16 | all-reduce | flops 1 | bytes 8 | tf_op jit(solution)/shard_map/psum | solution.py:48
  345.9 3.1 psum.29
  349.0 11.2 %psum.30 = f32[]{:T(128)} all-reduce(f32[]{:T(128)} %psum.29), channel_id=1, replica_groups=mesh['list_0'=4,'list_1'=2,'fsdp_0'=4,'fsdp_1'=4] {'fsdp_0'}, use_global_device_ids=true, to_apply=%region_17.18 | all-reduce | flops 1 | bytes 8 | tf_op jit(solution)/shard_map/psum | solution.py:48
  360.2 9.8 %psum.31 = f32[]{:T(128)} all-reduce(f32[]{:T(128)} %psum.30), channel_id=1, replica_groups=mesh['list_0'=4,'list_1'=2,'fsdp_0'=4,'fsdp_1'=4] {'fsdp_1'}, use_global_device_ids=true, to_apply=%region_18.19 | all-reduce | flops 1 | bytes 8 | tf_op jit(solution)/shard_map/psum | solution.py:48
  370.0 0.8 slice_convert_fusion
  370.9 0.7 copy.74
  371.7 0.8 slice_convert_fusion.1
  372.4 0.6 reshape.858
  (75 shorter events, 6.2 us)
Async XLA Ops:
  7.2 5.9 %copy-start.7 = (f32[2048]{0:T(1024)S(1)}, f32[2048]{0:T(1024)}, u32[]{:S(2)}) copy-start(f32[2048]{0:T(1024)} %param.10) | copy-start | bytes 24580
  7.2 66.7 %all-gather.11.cloned.1.call-start = ((), (), s32[]{:S(2)}) async-start(), calls=%async_computation.5 | async-start | bytes 6684672 | tf_op jit(solution)/shard_map/all_gather | solution.py:163
  7.9 123.7 %all-gather.13.cloned.1.call-start = ((), (), s32[]{:S(2)}) async-start(), calls=%async_computation.6 | async-start | bytes 4456448 | tf_op jit(solution)/shard_map/all_gather | solution.py:164
  8.7 282.9 %reduce-scatter.4.cloned.1.call-start = ((), (), s32[]{:S(2)}) async-start(), calls=%async_computation.7 | async-start | bytes 7864320 | tf_op jit(solution)/shard_map/reduce_scatter | solution.py:55
  9.7 3.5 copy-start.1
  92.7 8.4 %copy-start.4 = (bf16[1024,256]{1,0:T(8,128)(2,1)S(1)}, bf16[1024,256]{1,0:T(8,128)(2,1)}, u32[]{:S(2)}) copy-start(bf16[1024,256]{1,0:T(8,128)(2,1)} %get-tuple-element.26) | copy-start | bytes 1572868
  92.7 8.8 %copy-start.3 = (bf16[16,64,4,64,1]{1,3,4,2,0:T(8,128)(2,1)S(1)}, bf16[16,64,4,64,1]{1,3,4,2,0:T(8,128)(2,1)}, u32[]{:S(2)}) copy-start(bf16[16,64,4,64,1]{1,3,4,2,0:T(8,128)(2,1)} %copy.78) | copy-start | bytes 1572868
  115.8 2.2 copy-start
  131.6 8.9 %copy-start.5 = (f32[2048]{0:T(1024)S(1)}, f32[2048]{0:T(1024)}, u32[]{:S(2)}) copy-start(f32[2048]{0:T(1024)} %param.14) | copy-start | bytes 24580
  131.6 8.9 %copy-start.6 = (f32[2048]{0:T(1024)S(1)}, f32[2048]{0:T(1024)}, u32[]{:S(2)}) copy-start(f32[2048]{0:T(1024)} %param.13) | copy-start | bytes 24580
  131.6 9.1 %copy-start.9 = (f32[16]{0:T(128)S(1)}, f32[16]{0:T(128)}, u32[]{:S(2)}) copy-start(f32[16]{0:T(128)} %param.15) | copy-start | bytes 196
  131.6 9.4 %copy-start.8 = (s32[16]{0:T(128)S(1)}, s32[16]{0:T(128)}, u32[]{:S(2)}) copy-start(s32[16]{0:T(128)} %param.16) | copy-start | bytes 196
  131.6 44.9 %copy-start.2 = (bf16[1024,2048]{1,0:T(8,128)(2,1)S(1)}, bf16[1024,2048]{1,0:T(8,128)(2,1)}, u32[]{:S(2)}) copy-start(bf16[1024,2048]{1,0:T(8,128)(2,1)} %all-gather.13.cloned.1.call-done) | copy-start | bytes 12582916
  228.8 101.5 %reduce-scatter.6.cloned.1.call-start = ((), (), s32[]{:S(2)}) async-start(), calls=%async_computation.8 | async-start | bytes 1966080 | tf_op jit(solution)/shard_map/reduce_scatter | solution.py:55
  305.5 20.1 %all-to-all-start.1 = ((bf16[16,16,2048]{2,1,0:T(8,128)(2,1)}), bf16[16,16,2048]{2,1,0:T(8,128)(2,1)S(1)}, u32[]{:S(2)}, u32[]{:S(2)}) async-start(bf16[16,16,2048]{2,1,0:T(8,128)(2,1)} %broadcast_in_dim.12), calls=%async_computation.3 | async-start | bytes 2097152 | tf_op jit(solution)/shard_map/all_to_all | solution.py:67
  309.2 60.8 %reduce-scatter.8.cloned.1.call-start = ((), (), s32[]{:S(2)}) async-start(), calls=%async_computation.9 | async-start | bytes 737280 | tf_op jit(solution)/shard_map/reduce_scatter | solution.py:86
Sparse Core Ops, SparseCore 0:
  10.2 63.6 all-gather.10
  76.0 50.9 all-gather.12
  228.9 62.6 reduce-scatter.3
  293.8 36.3 reduce-scatter.5
  333.6 31.6 reduce-scatter.7
where the time goes:
time: 387 us; the launch traced here: 380 us
  waiting for transfers between devices  142 us (37%)
  blocking collectives  82.7 us (21%)
  matrix products  63.1 us (16%)
  local copies, waits for them, and re-layouts  56.8 us (15%)
  other arithmetic  16 us (4%)
  between operations  15 us (4%)
    reduce_scatter x2, waiting for transfers between devices, own_rows(): so_far = lax.psum_scatter(so_far, axis, scatter_dimension=0, tiled=True)  67 us
    all_gather x1, waiting for transfers between devices, local(): lax.all_gather(w_qkv, FSDP, axis=0, tiled=True)  57.7 us
    psum x4, blocking collectives, by_axis(): value = lax.psum(value, axis)  35.3 us
    all_gather x4, blocking collectives, collected_together(): both, at, found = (lax.all_gather(jnp.concatenate(lines), axis), 0, {})  34.7 us
    all_to_all x1, waiting for transfers between devices, from_everyone(): return lax.all_to_all(copies, axis, split_axis=0, concat_axis=0, tiled=True)  16.2 us
    all_to_all x1, blocking collectives, local(): lax.all_to_all(attn_sum, FSDP, split_axis=1, concat_axis=0, tiled=True)  12.7 us
    reshape x2, local copies, waits for them, and re-layouts, attend(): projected[:, :width_q]  12.3 us
    dot_general x1, matrix products, local(): lax.dot_general(normal_rows, d_projected, (((0,), (0,)), ((), ())), prefe...  11.8 us
  transfers between devices with their start and end apart: 6, of which 4 were waited for; matrix products, arithmetic and copies ran while one was open for 18% of the time, Pallas kernels for 0%

commit v1 on v0

v1 whole, which is shorter than its diff:
```python
import functools

import jax
import jax.numpy as jnp
from jax import lax
from jax.experimental import pallas as pl
from jax.experimental.pallas import tpu as pltpu
from jax.sharding import Mesh
from jax.sharding import PartitionSpec as P

BF = jnp.bfloat16
F32 = jnp.float32
FSDP = ("x", "y")
LIST = ("z", "c")
ALL = ("z", "c", "x", "y")
EPS = 1e-05
SCALE = 64.0
TOKENS = 64
PASS = 16
ROWS = PASS * TOKENS
D = 2048
COLS = 1536
QW = 1024
KVW = 256
VMEM_CAP = 60 * 1024 * 1024


def mm(a, b, ca, cb):
    return lax.dot_general(a, b, (((ca,), (cb,)), ((), ())), preferred_element_type=F32)


def norm_rows(hidden, gain, normal, hsum):
    g = gain[...]

    @pl.loop(0, PASS)
    def _(p):
        at = pl.ds(pl.multiple_of(p * TOKENS, TOKENS), TOKENS)
        x = hidden[at, :].astype(F32)
        mean_square = jnp.mean(x * x, axis=1, keepdims=True)
        normal[at, :] = (x * lax.rsqrt(mean_square + EPS) * g).astype(BF)
        hsum[pl.ds(p, 1), :] = jnp.sum(x, axis=0, keepdims=True)


SIDES = (1, -1)


class Gather:
    def __init__(self, view, own, sems, across):
        self.view, self.own, self.sems, self.across = view, own, sems, across
        self.z, self.c, self.x, self.y = place()
        self.copies = {}

    def slot(self, half, near, far):
        dx, dy = (far, near) if half == 0 else (near, far)
        return (self.x + dx) % 4 * 4 + (self.y + dy) % 4

    def peer(self, half, stage, step):
        name = "yx"[(half + stage) % 2]
        return {name: ((self.y if name == "y" else self.x) + step) % 4}

    def go(self, key, src, dst, where):
        self.copies[key] = send(src, dst, self.sems, len(self.copies), where)

    def pass_on(self, half, near, far):
        slot = self.slot(half, near, far)
        if far == 0:
            for step in SIDES:
                ref = self.view(slot, half, None)
                self.go((half, 2, near, step), ref, ref, self.peer(half, 1, step))
        if self.across:
            ref = self.view(slot, half, None)
            self.go((half, 5, near, far), ref, ref, {"c": 1 - self.c})

    def relay(self, key, half, stage, slot, step):
        ref = self.view(slot, half, 0 if step == 1 else 1)
        self.go(key, ref, ref, self.peer(half, stage, step))

    def begin(self):
        for half in range(2):
            for stage, key in ((0, (half, 1)), (1, (half, 2, 0))):
                for step in SIDES:
                    self.go(
                        (*key, step),
                        self.own(half),
                        self.view(self.slot(half, 0, 0), half, None),
                        self.peer(half, stage, step),
                    )

    def near_sides(self):
        for half in range(2):
            for step in SIDES:
                self.copies[half, 1, step].wait_recv()
                self.relay((half, 3, step), half, 0, self.slot(half, -step, 0), step)
                self.pass_on(half, -step, 0)

    def near_opposite(self):
        for half in range(2):
            for step in SIDES:
                self.copies[half, 3, step].wait_recv()
            self.pass_on(half, 2, 0)

    def far_sides(self):
        for near in (0, 1, -1, 2):
            for half in range(2):
                for step in SIDES:
                    self.copies[half, 2, near, step].wait_recv()
                    slot = self.slot(half, near, -step)
                    self.relay((half, 4, near, step), half, 1, slot, step)
                    self.pass_on(half, near, -step)

    def far_opposite(self):
        for near in (0, 1, -1, 2):
            for half in range(2):
                for step in SIDES:
                    self.copies[half, 4, near, step].wait_recv()
                self.pass_on(half, near, 2)

    def across_sides(self):
        self.across_wait(lambda near, far: near != 2 and far != 2)

    def across_rest(self):
        self.across_wait(lambda near, far: near == 2 or far == 2)

    def across_wait(self, chosen):
        for key, copy in self.copies.items():
            if key[1] == 5 and chosen(key[2], key[3]):
                copy.wait_recv()

    def end(self):
        for copy in self.copies.values():
            copy.wait_send()


def plane_peers(x, y, c):
    return [{"x": (x + 1) % 4}, {"x": (x + 3) % 4}, {"y": (y + 1) % 4}, {"y": (y + 3) % 4}, {"c": 1 - c}]


def project_part(wt, normal, total, projected, slots, last):
    @pl.loop(0, 4)
    def _(n):
        at = pl.multiple_of(n * 256, 256)
        cols = [pl.ds(pl.multiple_of(s * 128, 128), 128) for s in slots]
        rhs = jnp.concatenate([normal[pl.ds(at, 256), col] for col in cols], axis=1)
        for m in range(2):
            rows = pl.ds(m * 768, 768)
            lhs = jnp.concatenate([wt[s, rows, :] for s in slots], axis=1)
            out = mm(lhs, rhs, 1, 1)
            if last:
                projected[rows, pl.ds(at, 256)] = (total[rows, pl.ds(at, 256)] + out).astype(BF)
            else:
                total[rows, pl.ds(at, 256)] = out


def project_body(hidden, gain, own, normal, hsum, projected, wt, total, send_sems, recv_sems):
    z, c, x, y = place()

    def rows_of(half, part):
        start, size = half * 384, 384
        if part is not None:
            start, size = start + part * 192, 192
        return pl.ds(pl.multiple_of(c * 768 + start, 64), size)

    gather = Gather(
        lambda slot, half, part: wt.at[slot, rows_of(half, part), :],
        lambda half: own.at[rows_of(half, None), :],
        (send_sems, recv_sems),
        True,
    )
    greet(plane_peers(x, y, c))
    gather.begin()
    wt[x * 4 + y] = own[...]
    norm_rows(hidden, gain, normal, hsum)
    gather.near_sides()
    gather.near_opposite()
    gather.far_sides()
    gather.across_sides()
    steps = [(0, 0), (0, 1), (0, -1), (1, 0), (-1, 0), (1, 1), (1, -1), (-1, 1)]
    early = [(x + i) % 4 * 4 + (y + j) % 4 for i, j in steps]
    every = [(i, j) for i in (0, 1, 2, -1) for j in (0, 1, 2, -1)]
    late = [(x + i) % 4 * 4 + (y + j) % 4 for i, j in every if (i, j) not in steps]
    project_part(wt, normal, total, projected, early, False)
    gather.far_opposite()
    gather.across_rest()
    project_part(wt, normal, total, projected, late, True)
    gather.end()


def halves_mask():
    return lax.broadcasted_iota(jnp.int32, (1, 512), 1) % 128 < 64


def side_by_side(block):
    return jnp.concatenate([block[r * 64 : (r + 1) * 64] for r in range(4)], axis=1)


def own_blocks(full, first):
    return jnp.where(first, full[:64], full[64:])


def both_blocks(part, first):
    zero = jnp.zeros_like(part)
    return jnp.concatenate([jnp.where(first, part, zero), jnp.where(first, zero, part)], axis=0)


def places(i):
    g, pair = i // 8, i % 8
    lanes = pl.ds(pl.multiple_of(pair * 128, 128), 128)
    q_rows = pl.ds(pl.multiple_of(g * 256, 256), 256)
    k_rows = pl.ds(pl.multiple_of(QW + g * 64, 64), 64)
    v_rows = pl.ds(pl.multiple_of(QW + KVW + g * 64, 64), 64)
    return g, lanes, q_rows, k_rows, v_rows


def segments():
    row = lax.broadcasted_iota(jnp.int32, (PASS, ROWS), 0)
    lane = lax.broadcasted_iota(jnp.int32, (PASS, ROWS), 1)
    return (lane // TOKENS == row).astype(F32).astype(BF)


def attend(projected, probs, attended, begin, end):
    @pl.loop(begin, end)
    def _(i):
        first = halves_mask()
        _, lanes, q_rows, k_rows, v_rows = places(i)
        q = side_by_side(projected[q_rows, lanes])
        k, v = projected[k_rows, lanes], projected[v_rows, lanes]
        scores = own_blocks(mm(k, q, 0, 0), first) * 0.125
        expo = jnp.exp(scores - jnp.max(scores, axis=0, keepdims=True))
        part = (expo * (1.0 / jnp.sum(expo, axis=0, keepdims=True))).astype(BF)
        probs[i] = part
        out = mm(v, both_blocks(part, first), 1, 0).astype(BF)
        for r in range(4):
            attended[pl.ds(pl.multiple_of(i // 8 * 256 + r * 64, 64), 64), lanes] = out[
                :, r * 128 : (r + 1) * 128
            ]


def attend_back(projected, probs, d_att, d_projected, begin, end):
    @pl.loop(begin, end)
    def _(i):
        first = halves_mask()
        g, lanes, q_rows, k_rows, v_rows = places(i)
        q = side_by_side(projected[q_rows, lanes])
        da = side_by_side(d_att[q_rows, lanes])
        k, v = projected[k_rows, lanes], projected[v_rows, lanes]
        part = probs[i]
        d_probs = own_blocks(mm(v, da, 0, 0), first)
        values = part.astype(F32)
        inner = jnp.sum(values * d_probs, axis=0, keepdims=True)
        d_scores = both_blocks((values * (d_probs - inner) * 0.125).astype(BF), first)
        dq = mm(k, d_scores, 1, 0).astype(BF)
        for r in range(4):
            d_projected[pl.ds(pl.multiple_of(g * 256 + r * 64, 64), 64), lanes] = dq[
                :, r * 128 : (r + 1) * 128
            ]
        d_projected[k_rows, lanes] = mm(q, d_scores, 1, 1).astype(BF)
        d_projected[v_rows, lanes] = mm(da, both_blocks(part, first), 1, 1).astype(BF)


def send(src, dst, sems, slot, where):
    copy = pltpu.make_async_remote_copy(
        src_ref=src,
        dst_ref=dst,
        send_sem=sems[0].at[slot],
        recv_sem=sems[1].at[slot],
        device_id=where,
        device_id_type=pl.DeviceIdType.MESH,
    )
    copy.start()
    return copy


def place():
    return tuple(lax.axis_index(a) for a in ALL)


def greet(peers):
    barrier = pltpu.get_barrier_semaphore()
    for where in peers:
        pl.semaphore_signal(barrier, inc=1, device_id=where, device_id_type=pl.DeviceIdType.MESH)
    pl.semaphore_wait(barrier, len(peers))


def axis_peers(name, at):
    return [{name: (at + j) % 4} for j in (1, 2, 3)]


def exchange(table, sems):
    z, c, x, y = place()
    group = z * 2 + c
    mine = (group * 4 + x) * 4 + y
    slot = 0
    for name, at, start, size in (
        ("y", y, mine, 1),
        ("x", x, mine - y, 4),
        ("c", c, group * 16, 16),
        ("z", z, z * 32, 32),
    ):
        peers = [{"c": 1 - c}] if name == "c" else axis_peers(name, at)
        block = table.at[pl.ds(start, size)]
        copies = [send(block, block, sems, slot + j, where) for j, where in enumerate(peers)]
        slot += len(peers)
        for copy in copies:
            copy.wait()


def listwise(table, lengths, mine):
    length_row = lengths[...].astype(F32)
    row = lax.broadcasted_iota(jnp.int32, (64, 64), 0)
    lane = lax.broadcasted_iota(jnp.int32, (64, 64), 1)
    ends = jnp.sum(jnp.where(lane <= row, length_row, 0.0), axis=1, keepdims=True)
    starts = jnp.sum(jnp.where(lane < row, length_row, 0.0), axis=1, keepdims=True)
    lanes = lax.broadcasted_iota(jnp.int32, (1, 128), 1).astype(F32)
    score, weight, member = [], [], []
    top = jnp.full((64, 128), -1e30, F32)
    labels = jnp.zeros((64, 128), F32)
    for r in range(16):
        both = table[8 * r]
        for j in range(1, 8):
            both = both + table[8 * r + j]
        score.append(both[:, :128])
        weight.append(both[:, 128:])
        position = lanes + 128.0 * r
        member.append(jnp.logical_and(position >= starts, position < ends))
        top = jnp.maximum(top, jnp.where(member[r], score[r], -1e30))
        labels = labels + jnp.where(member[r], weight[r], 0.0)
    peak = jnp.max(top, axis=1, keepdims=True)
    label_total = jnp.sum(labels, axis=1, keepdims=True)
    total = jnp.zeros((64, 128), F32)
    for r in range(16):
        total = total + jnp.exp(jnp.where(member[r], score[r] - peak, -1e30))
    log_norm = peak + jnp.log(jnp.sum(total, axis=1, keepdims=True))
    terms = jnp.zeros((1, 128), F32)
    own = jnp.zeros((1, 128), F32)
    for r in range(16):
        norm = jnp.sum(jnp.where(member[r], log_norm, 0.0), axis=0, keepdims=True)
        labels = jnp.sum(jnp.where(member[r], label_total, 0.0), axis=0, keepdims=True)
        log_prob = score[r] - norm
        target = weight[r] / labels
        terms = terms + target * log_prob
        d_score = SCALE * (jnp.exp(log_prob) - target)
        own = own + jnp.where(mine // 8 == r, d_score, 0.0)
    return -SCALE * jnp.sum(terms, axis=1, keepdims=True), own


def middle_body(
    projected, hsum, own, final_gain, w_score, prior, labels, lengths,
    probs, pair, d_att, loss,
    attended, blocks, table, send_sems, recv_sems, out_send_sems, out_recv_sems,
):
    z, c, x, y = place()

    def rows_of(half):
        return pl.ds(pl.multiple_of(c * 32 + half * 16, 16), 16)

    def cols_of(part):
        return pl.ds(0, 2048) if part is None else pl.ds(part * 1024, 1024)

    gather = Gather(
        lambda slot, half, part: blocks.at[slot, rows_of(half), cols_of(part)],
        lambda half: own.at[rows_of(half), :],
        (out_send_sems, out_recv_sems),
        True,
    )
    greet(axis_peers("y", y) + axis_peers("x", x) + [{"c": 1 - c}] + axis_peers("z", z))
    gather.begin()
    blocks[x * 4 + y] = own[...]
    attend(projected, probs, attended, 0, 8)
    gather.near_sides()
    attend(projected, probs, attended, 8, 16)
    gather.near_opposite()
    attend(projected, probs, attended, 16, 24)
    gather.far_sides()
    attend(projected, probs, attended, 24, 32)
    gather.far_opposite()
    gather.across_sides()
    gather.across_rest()
    w_out = blocks[...].reshape(QW, D)
    sums = mm(segments(), attended[...], 1, 1)
    high = sums.astype(BF)
    pair[:, D:] = high
    low = (sums - high.astype(F32)).astype(BF)
    mixed = mm(jnp.concatenate([high, low], axis=0), w_out, 1, 0)
    pooled = (hsum[...] + mixed[:16] + mixed[16:]) * (1.0 / TOKENS)
    inverse = lax.rsqrt(jnp.mean(pooled * pooled, axis=1, keepdims=True) + EPS)
    unit = pooled * inverse
    weight = final_gain[...] * w_score[...]
    score = jnp.sum(unit * weight, axis=1, keepdims=True) + prior[...]
    mine = ((z * 2 + c) * 4 + x) * 4 + y
    row = lax.broadcasted_iota(jnp.int32, (16, 128), 0)
    lane = lax.broadcasted_iota(jnp.int32, (16, 128), 1)
    here = lane == row + mine % 8 * 16
    label_weight = jnp.exp(labels[...].astype(F32))
    score_row = jnp.sum(jnp.where(here, score, 0.0), axis=0, keepdims=True)
    label_row = jnp.sum(jnp.where(here, label_weight, 0.0), axis=0, keepdims=True)
    table[mine] = jnp.concatenate([score_row, label_row], axis=1)
    exchange(table, (send_sems, recv_sems))
    loss_value, own = listwise(table, lengths, mine)
    loss[...] = loss_value
    d_score = jnp.sum(jnp.where(here, own, 0.0), axis=1, keepdims=True)
    d_unit = d_score * weight
    d_pooled = inverse * (d_unit - unit * jnp.mean(d_unit * unit, axis=1, keepdims=True))
    grads = (d_pooled * (1.0 / TOKENS)).astype(BF)
    pair[:, :D] = grads
    d_attended = mm(w_out, grads, 1, 1).astype(BF)
    d_att[...] = mm(d_attended, segments(), 1, 0).astype(BF)
    gather.end()


ORDER = (2, 1, -1, 0)


class Scatter:
    def __init__(self, blocks, slabs, first, second, third, fourth, sems):
        self.blocks, self.slabs, self.sems = blocks, slabs, sems
        self.first, self.second, self.third, self.fourth = first, second, third, fourth
        self.z, self.c, self.x, self.y = place()
        self.copies = {}

    def at(self, half, stage):
        return self.x if (half + stage) % 2 == 0 else self.y

    def go(self, key, src, dst, half, stage, step):
        name = "xy"[(half + stage) % 2]
        where = {name: (self.at(half, stage) + step) % 4}
        self.copies[key] = send(src, dst, self.sems, len(self.copies), where)

    def part(self, step):
        return pl.ds(0 if step == 1 else 192, 192)

    def wide_first(self, half):
        block = self.blocks.at[half, 2]
        for k, step in enumerate(SIDES):
            self.go((half, 1, step), block.at[:, self.part(step), :], self.first.at[half, k], half, 0, step)

    def wide_second(self, half, step):
        k = SIDES.index(step)
        self.copies[half, 1, step].wait_recv()
        rows = self.part(step)
        at = step % 4
        mine = self.blocks[half, at, :, rows, :].astype(F32)
        self.blocks[half, at, :, rows, :] = (mine + self.first[half, k].astype(F32)).astype(BF)
        self.go((half, 2, step), self.blocks.at[half, at], self.second.at[half, k], half, 0, step)

    def wide_last(self, half):
        total = self.blocks[half, 0].astype(F32)
        for k, step in enumerate(SIDES):
            self.copies[half, 2, step].wait_recv()
            total = total + self.second[half, k].astype(F32)
        self.slabs[half] = total.astype(BF)
        slab = self.slabs.at[half, (self.at(half, 1) + 2) % 4]
        for k, step in enumerate(SIDES):
            self.go((half, 3, step), slab.at[self.part(step), :], self.third.at[half, k], half, 1, step)

    def narrow_second(self, half):
        for k, step in enumerate(SIDES):
            self.copies[half, 3, step].wait_recv()
            rows = self.part(step)
            at = (self.at(half, 1) + step) % 4
            mine = self.slabs[half, at, rows, :].astype(F32)
            self.slabs[half, at, rows, :] = (mine + self.third[half, k].astype(F32)).astype(BF)
            self.go((half, 4, step), self.slabs.at[half, at], self.fourth.at[half, k], half, 1, step)

    def narrow_last(self, half):
        total = self.slabs[half, self.at(half, 1)].astype(F32)
        for k, step in enumerate(SIDES):
            self.copies[half, 4, step].wait_recv()
            total = total + self.fourth[half, k].astype(F32)
        return total

    def end(self):
        for copy in self.copies.values():
            copy.wait_send()


def outer_peers(z, c):
    return [
        {"z": (z + j) % 4, "c": (c + k) % 2} for j in range(4) for k in range(2) if (j, k) != (0, 0)
    ]


def gradient_body(
    projected, probs, d_att, normal, pair,
    grad_qkv, grad_out,
    d_projected, everyone, wide, outer, outer_in,
    leaving, arriving, blocks, slabs, first, second, third, fourth, layers, layers_in,
    pair_send, pair_recv, core_send, core_recv, ring_send, ring_recv, list_send, list_recv,
):
    z, c, x, y = place()

    def lanes_of(half, part):
        return pl.ds(half * 1536, 1536) if part is None else pl.ds(half * 1536 + part * 768, 768)

    gather = Gather(
        lambda slot, half, part: everyone.at[slot, :, lanes_of(half, part)],
        lambda half: pair.at[:, lanes_of(half, None)],
        (pair_send, pair_recv),
        False,
    )
    outers = outer_peers(z, c)
    greet(plane_peers(x, y, c)[:4] + outers)
    gather.begin()
    everyone[x * 4 + y] = pair[...]
    attend_back(projected, probs, d_att, d_projected, 0, 8)
    gather.near_sides()
    attend_back(projected, probs, d_att, d_projected, 8, 16)
    gather.near_opposite()
    attend_back(projected, probs, d_att, d_projected, 16, 24)
    gather.far_sides()
    attend_back(projected, probs, d_att, d_projected, 24, 32)
    gather.far_opposite()

    ring = Scatter(blocks, slabs, first, second, third, fourth, (ring_send, ring_recv))
    units = [(step, half) for step in ORDER for half in range(2)]
    swaps = {}

    def unit(step, half):
        if half == 0:
            start = pl.multiple_of((x + step) % 4 * 512, 512)
            rhs = normal[:, pl.ds(start, 512)]
        else:
            at = [pl.multiple_of((i * 4 + (y + step) % 4) * 128, 128) for i in range(4)]
            rhs = jnp.concatenate([normal[:, pl.ds(a, 128)] for a in at], axis=1)
        for parity, target in ((1 - c, leaving), (c, blocks)):
            starts = [pl.multiple_of((4 * half + 2 * i + parity) * 192, 64) for i in range(2)]
            lhs = jnp.concatenate([d_projected[pl.ds(s, 192), :] for s in starts], axis=0)
            out = mm(lhs, rhs, 1, 0).astype(BF)
            for j in range(4):
                target[half, step % 4, j] = out[:, j * 128 : (j + 1) * 128]
        swaps[step, half] = send(
            leaving.at[half, step % 4],
            arriving.at[half, step % 4],
            (core_send, core_recv),
            len(swaps),
            {"c": 1 - c},
        )

    def joined(step, half):
        swaps[step, half].wait_recv()
        at = step % 4
        mine = blocks[half, at].astype(F32)
        blocks[half, at] = (mine + arriving[half, at].astype(F32)).astype(BF)

    for n, (step, half) in enumerate(units):
        unit(step, half)
        if n:
            joined(*units[n - 1])
            if units[n - 1][0] == 2:
                ring.wide_first(units[n - 1][1])
        if n == 5:
            ring.wide_second(0, 1)
        if n == 6:
            ring.wide_second(1, 1)
            ring.wide_second(0, -1)
    joined(*units[-1])
    ring.wide_second(1, -1)

    f = x * 4 + y
    lanes = pl.ds(pl.multiple_of(D + f // 2 * 128, 128), 128)
    sums = everyone[:, :, lanes].reshape(256, 128)
    wide[...] = mm(sums, everyone[:, :, :D].reshape(256, D), 0, 0)
    mine = wide[pl.ds(pl.multiple_of(f % 2 * 64, 64), 64), :].astype(BF)
    for l in range(8):
        outer[l] = mine[:, l * 256 : (l + 1) * 256]
    out_copies = [
        send(outer.at[w["z"] * 2 + w["c"]], outer_in.at[k], (list_send, list_recv), k, w)
        for k, w in enumerate(outers)
    ]
    ring.wide_last(0)
    ring.wide_last(1)
    ring.narrow_second(0)
    ring.narrow_second(1)
    total = outer[z * 2 + c].astype(F32)
    for k, copy in enumerate(out_copies):
        copy.wait()
        total = total + outer_in[k].astype(F32)
    grad_out[...] = total
    for half in range(2):
        both = ring.narrow_last(half).astype(BF)
        layers[2 * half] = both[:192]
        layers[2 * half + 1] = both[192:]
    layer_copies = [
        send(layers.at[(z + j) % 4], layers_in.at[j - 1], (list_send, list_recv), 6 + j, {"z": (z + j) % 4})
        for j in (1, 2, 3)
    ]
    total = layers[z].astype(F32)
    for k, copy in enumerate(layer_copies):
        copy.wait()
        total = total + layers_in[k].astype(F32)
    grad_qkv[...] = total
    gather.end()
    ring.end()
    for copy in swaps.values():
        copy.wait_send()


def vm():
    return pl.BlockSpec(memory_space=pltpu.VMEM)


def shape(*dims, dtype=BF):
    return jax.ShapeDtypeStruct(dims, dtype)


def semaphores(count):
    return [pltpu.SemaphoreType.DMA((count,))] * 2


def local(hidden, norm_gain, w_qkv, w_out, final_gain, w_score, prior, labels, lengths):
    rows = hidden.reshape(ROWS, D)
    params = functools.partial(
        pltpu.CompilerParams, vmem_limit_bytes=VMEM_CAP, has_side_effects=True
    )
    normal, hsum, projected = pl.pallas_call(
        project_body,
        out_shape=(shape(ROWS, D), shape(PASS, D, dtype=F32), shape(COLS, ROWS)),
        in_specs=[vm()] * 3,
        out_specs=(vm(),) * 3,
        scratch_shapes=[pltpu.VMEM((16, COLS, 128), BF), pltpu.VMEM((COLS, ROWS), F32)]
        + semaphores(70),
        compiler_params=params(collective_id=0),
        name="project",
    )(rows, norm_gain.reshape(1, D), w_qkv.T)
    probs, pair, d_att, loss = pl.pallas_call(
        middle_body,
        out_shape=(
            shape(32, 64, 512),
            shape(PASS, D + QW),
            shape(QW, ROWS),
            shape(1, 1, dtype=F32),
        ),
        in_specs=[vm()] * 8,
        out_specs=(vm(),) * 4,
        scratch_shapes=[
            pltpu.VMEM((QW, ROWS), BF),
            pltpu.VMEM((16, 64, D), BF),
            pltpu.VMEM((128, 1, 256), F32),
        ]
        + semaphores(10)
        + semaphores(70),
        compiler_params=params(collective_id=1),
        name="middle",
    )(
        projected, hsum, w_out, final_gain.reshape(1, D), w_score.reshape(1, D),
        prior.reshape(PASS, 1), labels.reshape(PASS, 1), lengths.reshape(1, -1),
    )
    grad_qkv, grad_out = pl.pallas_call(
        gradient_body,
        out_shape=(shape(192, 128, dtype=F32), shape(64, 256, dtype=F32)),
        in_specs=[vm()] * 5,
        out_specs=(vm(),) * 2,
        scratch_shapes=[
            pltpu.VMEM((COLS, ROWS), BF),
            pltpu.VMEM((16, PASS, D + QW), BF),
            pltpu.VMEM((128, D), F32),
            pltpu.VMEM((8, 64, 256), BF),
            pltpu.VMEM((7, 64, 256), BF),
            pltpu.VMEM((2, 4, 4, 384, 128), BF),
            pltpu.VMEM((2, 4, 4, 384, 128), BF),
            pltpu.VMEM((2, 4, 4, 384, 128), BF),
            pltpu.VMEM((2, 4, 384, 128), BF),
            pltpu.VMEM((2, 2, 4, 192, 128), BF),
            pltpu.VMEM((2, 2, 4, 384, 128), BF),
            pltpu.VMEM((2, 2, 192, 128), BF),
            pltpu.VMEM((2, 2, 384, 128), BF),
            pltpu.VMEM((4, 192, 128), BF),
            pltpu.VMEM((3, 192, 128), BF),
        ]
        + semaphores(40)
        + semaphores(8)
        + semaphores(16)
        + semaphores(10),
        compiler_params=params(collective_id=2),
        name="gradient",
    )(projected, probs, d_att, normal, pair)
    return loss.reshape(()), grad_qkv.T, grad_out


def solution(mesh):
    torus = Mesh(mesh.devices.reshape(4, 2, 4, 4), ALL)
    in_specs = (
        P(ALL, None, None), P(), P(FSDP, None), P(FSDP, None), P(), P(), P(ALL), P(ALL), P(),
    )
    out_specs = (P(), P(FSDP, LIST), P(FSDP, LIST))
    return jax.shard_map(local, mesh=torus, in_specs=in_specs, out_specs=out_specs, check_vma=False)
```

time: 387 us -> 154 us (0.40); the launches traced: 380 us -> 154 us
  Pallas kernels: 0 us -> 144 us
  waiting for transfers between devices: 142 us -> 0 us
  blocking collectives: 82.7 us -> 0 us
  matrix products: 63.1 us -> 0 us
  local copies, waits for them, and re-layouts: 56.8 us -> 7.58 us
  other arithmetic: 16 us -> 0 us
  between operations: 15 us -> 2.47 us
    pallas_call x0 -> x3, Pallas kernels: none -> 144 us  [the longest x1 61 us: local(): pl.pallas_call(gradient_body, out_shape=(shape(192, 128, dtype=F32), shap...]
    reduce_scatter x3 -> x0, waiting for transfers between devices: 67 us -> none  [the longest x2 67 us: own_rows(): so_far = lax.psum_scatter(so_far, axis, scatter_dimension=0, tiled=True)]
    all_gather x2 -> x0, waiting for transfers between devices: 57.7 us -> none  [the longest x1 57.7 us: local(): lax.all_gather(w_qkv, FSDP, axis=0, tiled=True)]
    dot_general x10 -> x0, matrix products: 54.5 us -> none  [the longest x1 11.8 us: local(): lax.dot_general(normal_rows, d_projected, (((0,), (0,)), ((), ())), prefe...]
    psum x4 -> x0, blocking collectives: 35.3 us -> none  [by_axis(): value = lax.psum(value, axis)]
    all_gather x4 -> x0, blocking collectives: 34.7 us -> none  [collected_together(): both, at, found = (lax.all_gather(jnp.concatenate(lines), axis), 0, {})]
    reshape x11 -> x2, local copies, waits for them, and re-layouts: 26.5 us -> 2.66 us  [the longest x1 1.33 us: local(): prior.reshape(PASS, 1)]
    convert_element_type x6 -> x0, local copies, waits for them, and re-layouts: 16.4 us -> none  [the longest x1 7.63 us: attend_back(): d_query = jnp.einsum('bgrqk,bkge->bqgre', d_scores, key_part, preferred_e...]
  transfers between devices with their start and end apart: 6 -> 0, of which waited for: 4 -> 0; matrix products, arithmetic and copies ran while one was open for 18% -> 0% of each run, Pallas kernels for 0% -> 0%
where the time goes in v1:
time: 154 us
  Pallas kernels  144 us (94%)
  local copies, waits for them, and re-layouts  7.58 us (5%)
  between operations  2.47 us (2%)
    pallas_call x1, Pallas kernels, local(): pl.pallas_call(gradient_body, out_shape=(shape(192, 128, dtype=F32), shap...  61 us
    pallas_call x1, Pallas kernels, local(): pl.pallas_call(middle_body, out_shape=(shape(32, 64, 512), shape(PASS, D...  46.2 us
    pallas_call x1, Pallas kernels, local(): pl.pallas_call(project_body, out_shape=(shape(ROWS, D), shape(PASS, D, dt...  36.7 us
    unnamed x3, local copies, waits for them, and re-layouts  4.92 us

profile of v1, /device:TPU:0, one launch (start us, length us, event | category | flops | bytes accessed | tf_op | source)
XLA Modules:
  0.0 154.1 jit_solution(11159466425977785944)
XLA Ops:
  0.6 1.3 copy.13.prior
  2.0 1.3 copy.14.labels
  3.3 1.9 %copy.12 = bf16[128,1536]{0,1:T(8,128)(2,1)} copy(bf16[128,1536]{1,0:T(8,128)(2,1)} %param.11) | data formatting | bytes 786432 | tf_op args[2]
  5.2 36.7 %project.1 = (bf16[1024,2048]{1,0:T(8,128)(2,1)}, f32[16,2048]{1,0:T(8,128)}, bf16[1536,1024]{1,0:T(8,128)(2,1)}) custom-call(bf16[1024,2048]{1,0:T(8,128)(2,1)} %bitcast.10, f32[1,2048]{1,0:T(1,128)} %bitcast.13, bf16[1536,128]{1,0:T(8,128)(2,1)} %bitcast.11), custom_call_target="tpu_custom_call" | custom-call | tf_op jit(solution)/shard_map/project/pallas_call | solution.py:614
  41.9 46.2 %middle.1 = (bf16[32,64,512]{2,1,0:T(8,128)(2,1)}, bf16[16,3072]{1,0:T(8,128)(2,1)}, bf16[1024,1024]{1,0:T(8,128)(2,1)}, f32[1,1]{1,0:T(1,128)}) custom-call(bf16[1536,1024]{1,0:T(8,128)(2,1)} %get-tuple-element.12.projected, f32[16,2048]{1,0:T(8,128)} %get-tuple-element.13.hsum, bf16[64,2048]{1,0:T(8,128)(2,1)} %own.1, f32[1,2048]{1,0:T(1,128)} %bitcast.14, ...), custom_call_target="tpu_custom_call" | custom-call | tf_op jit(solution)/shard_map/middle/pallas_call | solution.py:624
  88.2 61.0 %gradient.1 = (f32[192,128]{1,0:T(8,128)}, f32[64,256]{1,0:T(8,128)}) custom-call(bf16[1536,1024]{1,0:T(8,128)(2,1)} %get-tuple-element.12.projected, bf16[32,64,512]{2,1,0:T(8,128)(2,1)} %get-tuple-element.15.probs, bf16[1024,1024]{1,0:T(8,128)(2,1)} %get-tuple-element.16.d_att, bf16[1024,2048]{1,0:T(8,128)(2,1)} %get-tuple-element.17.normal, ...), custom_call_target="tpu_custom_call" | custom-call | tf_op jit(solution)/shard_map/gradient/pallas_call | solution.py:647
  149.9 1.5 copy.19
  151.5 1.5 copy.20

commit v2 on v1

--- a/solution.py
+++ b/solution.py
@@ -1,5 +1,3 @@
-import functools
-
 import jax
 import jax.numpy as jnp
 from jax import lax
@@ -22,7 +20,7 @@
 COLS = 1536
 QW = 1024
 KVW = 256
-VMEM_CAP = 60 * 1024 * 1024
+VMEM_CAP = 63 * 1024 * 1024
 
 
 def mm(a, b, ca, cb):
@@ -149,40 +147,6 @@
                 projected[rows, pl.ds(at, 256)] = (total[rows, pl.ds(at, 256)] + out).astype(BF)
             else:
                 total[rows, pl.ds(at, 256)] = out
-
-
-def project_body(hidden, gain, own, normal, hsum, projected, wt, total, send_sems, recv_sems):
-    z, c, x, y = place()
-
-    def rows_of(half, part):
-        start, size = half * 384, 384
-        if part is not None:
-            start, size = start + part * 192, 192
-        return pl.ds(pl.multiple_of(c * 768 + start, 64), size)
-
-    gather = Gather(
-        lambda slot, half, part: wt.at[slot, rows_of(half, part), :],
-        lambda half: own.at[rows_of(half, None), :],
-        (send_sems, recv_sems),
-        True,
-    )
-    greet(plane_peers(x, y, c))
-    gather.begin()
-    wt[x * 4 + y] = own[...]
-    norm_rows(hidden, gain, normal, hsum)
-    gather.near_sides()
-    gather.near_opposite()
-    gather.far_sides()
-    gather.across_sides()
-    steps = [(0, 0), (0, 1), (0, -1), (1, 0), (-1, 0), (1, 1), (1, -1), (-1, 1)]
-    early = [(x + i) % 4 * 4 + (y + j) % 4 for i, j in steps]
-    every = [(i, j) for i in (0, 1, 2, -1) for j in (0, 1, 2, -1)]
-    late = [(x + i) % 4 * 4 + (y + j) % 4 for i, j in every if (i, j) not in steps]
-    project_part(wt, normal, total, projected, early, False)
-    gather.far_opposite()
-    gather.across_rest()
-    project_part(wt, normal, total, projected, late, True)
-    gather.end()
 
 
 def halves_mask():
@@ -285,26 +249,31 @@
     return [{name: (at + j) % 4} for j in (1, 2, 3)]
 
 
-def exchange(table, sems):
-    z, c, x, y = place()
-    group = z * 2 + c
-    mine = (group * 4 + x) * 4 + y
-    slot = 0
-    for name, at, start, size in (
-        ("y", y, mine, 1),
-        ("x", x, mine - y, 4),
-        ("c", c, group * 16, 16),
-        ("z", z, z * 32, 32),
-    ):
-        peers = [{"c": 1 - c}] if name == "c" else axis_peers(name, at)
-        block = table.at[pl.ds(start, size)]
-        copies = [send(block, block, sems, slot + j, where) for j, where in enumerate(peers)]
-        slot += len(peers)
-        for copy in copies:
+class Exchange:
+    def __init__(self, table, sems):
+        z, c, x, y = place()
+        group = z * 2 + c
+        mine = (group * 4 + x) * 4 + y
+        self.table, self.sems, self.used, self.copies = table, sems, 0, []
+        self.stages = [
+            (axis_peers("y", y), mine, 1),
+            (axis_peers("x", x), mine - y, 4),
+            ([{"c": 1 - c}], group * 16, 16),
+            (axis_peers("z", z), z * 32, 32),
+        ]
+
+    def start(self, stage):
+        peers, start, size = self.stages[stage]
+        block = self.table.at[pl.ds(start, size)]
+        self.copies = [send(block, block, self.sems, self.used + j, w) for j, w in enumerate(peers)]
+        self.used += len(peers)
+
+    def wait(self):
+        for copy in self.copies:
             copy.wait()
 
 
-def listwise(table, lengths, mine):
+def listwise(table, lengths, group):
     length_row = lengths[...].astype(F32)
     row = lax.broadcasted_iota(jnp.int32, (64, 64), 0)
     lane = lax.broadcasted_iota(jnp.int32, (64, 64), 1)
@@ -331,7 +300,7 @@
         total = total + jnp.exp(jnp.where(member[r], score[r] - peak, -1e30))
     log_norm = peak + jnp.log(jnp.sum(total, axis=1, keepdims=True))
     terms = jnp.zeros((1, 128), F32)
-    own = jnp.zeros((1, 128), F32)
+    own = [jnp.zeros((1, 128), F32)] * 2
     for r in range(16):
         norm = jnp.sum(jnp.where(member[r], log_norm, 0.0), axis=0, keepdims=True)
         labels = jnp.sum(jnp.where(member[r], label_total, 0.0), axis=0, keepdims=True)
@@ -339,72 +308,8 @@
         target = weight[r] / labels
         terms = terms + target * log_prob
         d_score = SCALE * (jnp.exp(log_prob) - target)
-        own = own + jnp.where(mine // 8 == r, d_score, 0.0)
+        own[r % 2] = own[r % 2] + jnp.where(group == r // 2, d_score, 0.0)
     return -SCALE * jnp.sum(terms, axis=1, keepdims=True), own
-
-
-def middle_body(
-    projected, hsum, own, final_gain, w_score, prior, labels, lengths,
-    probs, pair, d_att, loss,
-    attended, blocks, table, send_sems, recv_sems, out_send_sems, out_recv_sems,
-):
-    z, c, x, y = place()
-
-    def rows_of(half):
-        return pl.ds(pl.multiple_of(c * 32 + half * 16, 16), 16)
-
-    def cols_of(part):
-        return pl.ds(0, 2048) if part is None else pl.ds(part * 1024, 1024)
-
-    gather = Gather(
-        lambda slot, half, part: blocks.at[slot, rows_of(half), cols_of(part)],
-        lambda half: own.at[rows_of(half), :],
-        (out_send_sems, out_recv_sems),
-        True,
-    )
-    greet(axis_peers("y", y) + axis_peers("x", x) + [{"c": 1 - c}] + axis_peers("z", z))
-    gather.begin()
-    blocks[x * 4 + y] = own[...]
-    attend(projected, probs, attended, 0, 8)
-    gather.near_sides()
-    attend(projected, probs, attended, 8, 16)
-    gather.near_opposite()
-    attend(projected, probs, attended, 16, 24)
-    gather.far_sides()
-    attend(projected, probs, attended, 24, 32)
-    gather.far_opposite()
-    gather.across_sides()
-    gather.across_rest()
-    w_out = blocks[...].reshape(QW, D)
-    sums = mm(segments(), attended[...], 1, 1)
-    high = sums.astype(BF)
-    pair[:, D:] = high
-    low = (sums - high.astype(F32)).astype(BF)
-    mixed = mm(jnp.concatenate([high, low], axis=0), w_out, 1, 0)
-    pooled = (hsum[...] + mixed[:16] + mixed[16:]) * (1.0 / TOKENS)
-    inverse = lax.rsqrt(jnp.mean(pooled * pooled, axis=1, keepdims=True) + EPS)
-    unit = pooled * inverse
-    weight = final_gain[...] * w_score[...]
-    score = jnp.sum(unit * weight, axis=1, keepdims=True) + prior[...]
-    mine = ((z * 2 + c) * 4 + x) * 4 + y
-    row = lax.broadcasted_iota(jnp.int32, (16, 128), 0)
-    lane = lax.broadcasted_iota(jnp.int32, (16, 128), 1)
-    here = lane == row + mine % 8 * 16
-    label_weight = jnp.exp(labels[...].astype(F32))
-    score_row = jnp.sum(jnp.where(here, score, 0.0), axis=0, keepdims=True)
-    label_row = jnp.sum(jnp.where(here, label_weight, 0.0), axis=0, keepdims=True)
-    table[mine] = jnp.concatenate([score_row, label_row], axis=1)
-    exchange(table, (send_sems, recv_sems))
-    loss_value, own = listwise(table, lengths, mine)
-    loss[...] = loss_value
-    d_score = jnp.sum(jnp.where(here, own, 0.0), axis=1, keepdims=True)
-    d_unit = d_score * weight
-    d_pooled = inverse * (d_unit - unit * jnp.mean(d_unit * unit, axis=1, keepdims=True))
-    grads = (d_pooled * (1.0 / TOKENS)).astype(BF)
-    pair[:, :D] = grads
-    d_attended = mm(w_out, grads, 1, 1).astype(BF)
-    d_att[...] = mm(d_attended, segments(), 1, 0).astype(BF)
-    gather.end()
 
 
 ORDER = (2, 1, -1, 0)
@@ -479,36 +384,151 @@
     ]
 
 
-def gradient_body(
-    projected, probs, d_att, normal, pair,
-    grad_qkv, grad_out,
+def as_column(row):
+    count = row.shape[1]
+    same = lax.broadcasted_iota(jnp.int32, (count, count), 0) == lax.broadcasted_iota(
+        jnp.int32, (count, count), 1
+    )
+    return jnp.sum(jnp.where(same, row, 0.0), axis=1, keepdims=True)
+
+
+def whole_body(
+    hidden, gain, w_qkv, w_out_own, final_gain, w_score, prior, labels, lengths,
+    loss, grad_qkv, grad_out,
+    normal, hsum, wt, total_f, projected, probs, attended, w_blocks, table, pair,
     d_projected, everyone, wide, outer, outer_in,
     leaving, arriving, blocks, slabs, first, second, third, fourth, layers, layers_in,
+    qkv_send, qkv_recv, out_send, out_recv, table_send, table_recv,
     pair_send, pair_recv, core_send, core_recv, ring_send, ring_recv, list_send, list_recv,
 ):
     z, c, x, y = place()
-
-    def lanes_of(half, part):
+    d_att = attended
+    f = x * 4 + y
+    group = z * 2 + c
+
+    def qkv_rows(half, part, core):
+        start, size = half * 384, 384
+        if part is not None:
+            start, size = start + part * 192, 192
+        return pl.ds(pl.multiple_of(core * 768 + start, 64), size)
+
+    def out_rows(half):
+        return pl.ds(pl.multiple_of(c * 32 + half * 16, 16), 16)
+
+    def out_cols(part):
+        return pl.ds(0, D) if part is None else pl.ds(part * 1024, 1024)
+
+    def pair_cols(half, part):
         return pl.ds(half * 1536, 1536) if part is None else pl.ds(half * 1536 + part * 768, 768)
 
-    gather = Gather(
-        lambda slot, half, part: everyone.at[slot, :, lanes_of(half, part)],
-        lambda half: pair.at[:, lanes_of(half, None)],
+    qkv_gather = Gather(
+        lambda slot, half, part: wt.at[slot, qkv_rows(half, part, c), :],
+        lambda half: wt.at[f, qkv_rows(half, None, c), :],
+        (qkv_send, qkv_recv),
+        True,
+    )
+    out_gather = Gather(
+        lambda slot, half, part: w_blocks.at[slot, out_rows(half), out_cols(part)],
+        lambda half: w_out_own.at[out_rows(half), :],
+        (out_send, out_recv),
+        True,
+    )
+    pair_gather = Gather(
+        lambda slot, half, part: everyone.at[slot, :, pair_cols(half, part)],
+        lambda half: pair.at[:, pair_cols(half, None)],
         (pair_send, pair_recv),
         False,
     )
+    scores = Exchange(table, (table_send, table_recv))
     outers = outer_peers(z, c)
-    greet(plane_peers(x, y, c)[:4] + outers)
-    gather.begin()
-    everyone[x * 4 + y] = pair[...]
+
+    def turned(core):
+        for half in range(2):
+            cols = pl.ds(pl.multiple_of(core * 768 + half * 384, 128), 384)
+            wt[f, qkv_rows(half, None, core), :] = w_qkv[:, cols].T
+
+    turned(c)
+    greet(axis_peers("y", y) + axis_peers("x", x) + outers)
+    qkv_gather.begin()
+    turned(1 - c)
+    w_blocks[f] = w_out_own[...]
+    norm_rows(hidden, gain, normal, hsum)
+    qkv_gather.near_sides()
+    qkv_gather.near_opposite()
+    qkv_gather.far_sides()
+    out_gather.begin()
+    qkv_gather.across_sides()
+    steps = [(0, 0), (0, 1), (0, -1), (1, 0), (-1, 0), (1, 1), (1, -1), (-1, 1)]
+    early = [(x + i) % 4 * 4 + (y + j) % 4 for i, j in steps]
+    every = [(i, j) for i in (0, 1, 2, -1) for j in (0, 1, 2, -1)]
+    late = [(x + i) % 4 * 4 + (y + j) % 4 for i, j in every if (i, j) not in steps]
+    project_part(wt, normal, total_f, projected, early, False)
+    qkv_gather.far_opposite()
+    out_gather.near_sides()
+    qkv_gather.across_rest()
+    project_part(wt, normal, total_f, projected, late, True)
+    out_gather.near_opposite()
+    attend(projected, probs, attended, 0, 8)
+    out_gather.far_sides()
+    attend(projected, probs, attended, 8, 24)
+    out_gather.far_opposite()
+    attend(projected, probs, attended, 24, 32)
+    out_gather.across_sides()
+    out_gather.across_rest()
+
+    w_out = w_blocks[...].reshape(QW, D)
+    sums = mm(segments(), attended[...], 1, 1)
+    high = sums.astype(BF)
+    low = (sums - high.astype(F32)).astype(BF)
+    mixed = mm(jnp.concatenate([high, low], axis=0), w_out, 1, 0)
+    pooled = (hsum[...] + mixed[:16] + mixed[16:]) * (1.0 / TOKENS)
+    inverse = lax.rsqrt(jnp.mean(pooled * pooled, axis=1, keepdims=True) + EPS)
+    unit = pooled * inverse
+    weight = final_gain[...] * w_score[...]
+    score = jnp.sum(unit * weight, axis=1, keepdims=True) + as_column(prior[...])
+    mine = group * 16 + f
+    row = lax.broadcasted_iota(jnp.int32, (16, 128), 0)
+    lane = lax.broadcasted_iota(jnp.int32, (16, 128), 1)
+    here = lane == row + mine % 8 * 16
+    label_weight = jnp.exp(as_column(labels[...].astype(F32)))
+    score_row = jnp.sum(jnp.where(here, score, 0.0), axis=0, keepdims=True)
+    label_row = jnp.sum(jnp.where(here, label_weight, 0.0), axis=0, keepdims=True)
+    table[mine] = jnp.concatenate([score_row, label_row], axis=1)
+    scores.start(0)
+    slope = inverse * (weight - unit * jnp.mean(weight * unit, axis=1, keepdims=True))
+    slope = (slope * (1.0 / TOKENS)).astype(BF)
+    pair[:, :D] = slope
+    pair[:, D:] = high
+    pair_gather.begin()
+    everyone[f] = pair[...]
+    d_attended = mm(w_out, slope, 1, 1).astype(BF)
+    d_att[...] = mm(d_attended, segments(), 1, 0).astype(BF)
+    scores.wait()
+    scores.start(1)
     attend_back(projected, probs, d_att, d_projected, 0, 8)
-    gather.near_sides()
-    attend_back(projected, probs, d_att, d_projected, 8, 16)
-    gather.near_opposite()
-    attend_back(projected, probs, d_att, d_projected, 16, 24)
-    gather.far_sides()
-    attend_back(projected, probs, d_att, d_projected, 24, 32)
-    gather.far_opposite()
+    scores.wait()
+    scores.start(2)
+    pair_gather.near_sides()
+    attend_back(projected, probs, d_att, d_projected, 8, 12)
+    scores.wait()
+    scores.start(3)
+    attend_back(projected, probs, d_att, d_projected, 12, 20)
+    pair_gather.near_opposite()
+    attend_back(projected, probs, d_att, d_projected, 20, 32)
+    scores.wait()
+    pair_gather.far_sides()
+    loss_value, factors = listwise(table, lengths, group)
+    loss[...] = loss_value
+    own = jnp.where(f // 8 == 0, factors[0], factors[1])
+    factor = jnp.sum(jnp.where(here, own, 0.0), axis=1, keepdims=True)
+    token = lax.broadcasted_iota(jnp.int32, (PASS, ROWS), 1) // TOKENS
+    passage = lax.broadcasted_iota(jnp.int32, (PASS, ROWS), 0)
+    factor_row = jnp.sum(jnp.where(token == passage, factor, 0.0), axis=0, keepdims=True)
+
+    @pl.loop(0, 12)
+    def _(i):
+        at = pl.ds(pl.multiple_of(i * 128, 128), 128)
+        d_projected[at, :] = (d_projected[at, :].astype(F32) * factor_row).astype(BF)
 
     ring = Scatter(blocks, slabs, first, second, third, fourth, (ring_send, ring_recv))
     units = [(step, half) for step in ORDER for half in range(2)]
@@ -555,9 +575,10 @@
     joined(*units[-1])
     ring.wide_second(1, -1)
 
-    f = x * 4 + y
+    pair_gather.far_opposite()
     lanes = pl.ds(pl.multiple_of(D + f // 2 * 128, 128), 128)
-    sums = everyone[:, :, lanes].reshape(256, 128)
+    group_factor = jnp.concatenate([as_column(factors[0]), as_column(factors[1])], axis=0)
+    sums = (everyone[:, :, lanes].reshape(256, 128).astype(F32) * group_factor).astype(BF)
     wide[...] = mm(sums, everyone[:, :, :D].reshape(256, D), 0, 0)
     mine = wide[pl.ds(pl.multiple_of(f % 2 * 64, 64), 64), :].astype(BF)
     for l in range(8):
@@ -587,8 +608,10 @@
     for k, copy in enumerate(layer_copies):
         copy.wait()
         total = total + layers_in[k].astype(F32)
-    grad_qkv[...] = total
-    gather.end()
+    grad_qkv[...] = total.T
+    qkv_gather.end()
+    out_gather.end()
+    pair_gather.end()
     ring.end()
     for copy in swaps.values():
         copy.wait_send()
@@ -607,49 +630,26 @@
 
 
 def local(hidden, norm_gain, w_qkv, w_out, final_gain, w_score, prior, labels, lengths):
-    rows = hidden.reshape(ROWS, D)
-    params = functools.partial(
-        pltpu.CompilerParams, vmem_limit_bytes=VMEM_CAP, has_side_effects=True
-    )
-    normal, hsum, projected = pl.pallas_call(
-        project_body,
-        out_shape=(shape(ROWS, D), shape(PASS, D, dtype=F32), shape(COLS, ROWS)),
-        in_specs=[vm()] * 3,
+    loss, grad_qkv, grad_out = pl.pallas_call(
+        whole_body,
+        out_shape=(
+            shape(1, 1, dtype=F32),
+            shape(128, 192, dtype=F32),
+            shape(64, 256, dtype=F32),
+        ),
+        in_specs=[vm()] * 9,
         out_specs=(vm(),) * 3,
-        scratch_shapes=[pltpu.VMEM((16, COLS, 128), BF), pltpu.VMEM((COLS, ROWS), F32)]
-        + semaphores(70),
-        compiler_params=params(collective_id=0),
-        name="project",
-    )(rows, norm_gain.reshape(1, D), w_qkv.T)
-    probs, pair, d_att, loss = pl.pallas_call(
-        middle_body,
-        out_shape=(
-            shape(32, 64, 512),
-            shape(PASS, D + QW),
-            shape(QW, ROWS),
-            shape(1, 1, dtype=F32),
-        ),
-        in_specs=[vm()] * 8,
-        out_specs=(vm(),) * 4,
         scratch_shapes=[
+            pltpu.VMEM((ROWS, D), BF),
+            pltpu.VMEM((PASS, D), F32),
+            pltpu.VMEM((16, COLS, 128), BF),
+            pltpu.VMEM((COLS, ROWS), F32),
+            pltpu.VMEM((COLS, ROWS), BF),
+            pltpu.VMEM((32, 64, 512), BF),
             pltpu.VMEM((QW, ROWS), BF),
             pltpu.VMEM((16, 64, D), BF),
             pltpu.VMEM((128, 1, 256), F32),
-        ]
-        + semaphores(10)
-        + semaphores(70),
-        compiler_params=params(collective_id=1),
-        name="middle",
-    )(
-        projected, hsum, w_out, final_gain.reshape(1, D), w_score.reshape(1, D),
-        prior.reshape(PASS, 1), labels.reshape(PASS, 1), lengths.reshape(1, -1),
-    )
-    grad_qkv, grad_out = pl.pallas_call(
-        gradient_body,
-        out_shape=(shape(192, 128, dtype=F32), shape(64, 256, dtype=F32)),
-        in_specs=[vm()] * 5,
-        out_specs=(vm(),) * 2,
-        scratch_shapes=[
+            pltpu.VMEM((PASS, D + QW), BF),
             pltpu.VMEM((COLS, ROWS), BF),
             pltpu.VMEM((16, PASS, D + QW), BF),
             pltpu.VMEM((128, D), F32),
@@ -666,14 +666,23 @@
             pltpu.VMEM((4, 192, 128), BF),
             pltpu.VMEM((3, 192, 128), BF),
         ]
+        + semaphores(70)
+        + semaphores(70)
+        + semaphores(10)
         + semaphores(40)
         + semaphores(8)
         + semaphores(16)
         + semaphores(10),
-        compiler_params=params(collective_id=2),
-        name="gradient",
-    )(projected, probs, d_att, normal, pair)
-    return loss.reshape(()), grad_qkv.T, grad_out
+        compiler_params=pltpu.CompilerParams(
+            vmem_limit_bytes=VMEM_CAP, has_side_effects=True, collective_id=0
+        ),
+        name="whole",
+    )(
+        hidden.reshape(ROWS, D), norm_gain.reshape(1, D), w_qkv, w_out,
+        final_gain.reshape(1, D), w_score.reshape(1, D),
+        prior.reshape(1, PASS), labels.reshape(1, PASS), lengths.reshape(1, -1),
+    )
+    return loss.reshape(()), grad_qkv, grad_out
 
 
 def solution(mesh):

time: 154 us -> 120 us (0.78)
  Pallas kernels: 144 us -> 114 us
  local copies, waits for them, and re-layouts: 7.58 us -> 3.12 us
    pallas_call x3 -> x1, Pallas kernels: 144 us -> 114 us  [local(): pl.pallas_call(whole_body, out_shape=(shape(1, 1, dtype=F32), shape(128,...]
    reshape x2 -> x0, local copies, waits for them, and re-layouts: 2.66 us -> none  [the longest x1 1.33 us: local(): prior.reshape(PASS, 1)]
    unnamed x3 -> x2, local copies, waits for them, and re-layouts: 4.92 us -> 3.12 us
where the time goes in v2:
time: 120 us; the launch traced here: 119 us
  Pallas kernels  114 us (95%)
  local copies, waits for them, and re-layouts  3.12 us (3%)
  between operations  2.41 us (2%)
    pallas_call x1, Pallas kernels, local(): pl.pallas_call(whole_body, out_shape=(shape(1, 1, dtype=F32), shape(128,...  114 us
    unnamed x2, local copies, waits for them, and re-layouts  3.12 us

profile of v2, /device:TPU:0, one launch (start us, length us, event | category | flops | bytes accessed | tf_op | source)
XLA Modules:
  0.0 119.4 jit_solution(2648132472921935427)
XLA Ops:
  0.6 113.9 %whole.1 = (f32[1,1]{1,0:T(1,128)}, f32[128,192]{1,0:T(8,128)}, f32[64,256]{1,0:T(8,128)}) custom-call(bf16[1024,2048]{1,0:T(8,128)(2,1)} %bitcast.8, f32[1,2048]{1,0:T(1,128)} %bitcast.9, bf16[128,1536]{1,0:T(8,128)(2,1)} %w_qkv.1, bf16[64,2048]{1,0:T(8,128)(2,1)} %w_out_own.1, f32[1,2048]{1,0:T(1,128)} %bitcast.10, f32[1,2048]{1,0:T(1,128)} %bitcast.11, ...), custom_call_target="tpu_custom_call" | custom-call | tf_op jit(solution)/shard_map/whole/pallas_call | solution.py:633
  114.5 1.6 %copy.12 = f32[128,192]{0,1:T(8,128)} copy(f32[128,192]{1,0:T(8,128)} %get-tuple-element.10) | data formatting | bytes 196608
  116.8 1.5 %copy.16 = f32[64,256]{1,0:T(8,128)} copy(f32[64,256]{1,0:T(8,128)} %get-tuple-element.17) | data formatting | bytes 131072

commit v3 on v2

--- a/solution.py
+++ b/solution.py
@@ -133,8 +133,8 @@
     return [{"x": (x + 1) % 4}, {"x": (x + 3) % 4}, {"y": (y + 1) % 4}, {"y": (y + 3) % 4}, {"c": 1 - c}]
 
 
-def project_part(wt, normal, total, projected, slots, last):
-    @pl.loop(0, 4)
+def project_part(wt, normal, total, projected, slots, last, begin, end):
+    @pl.loop(begin, end)
     def _(n):
         at = pl.multiple_of(n * 256, 256)
         cols = [pl.ds(pl.multiple_of(s * 128, 128), 128) for s in slots]
@@ -181,44 +181,57 @@
     return (lane // TOKENS == row).astype(F32).astype(BF)
 
 
+UNROLL = 4
+
+
 def attend(projected, probs, attended, begin, end):
-    @pl.loop(begin, end)
-    def _(i):
+    @pl.loop(begin // UNROLL, end // UNROLL)
+    def _(t):
         first = halves_mask()
-        _, lanes, q_rows, k_rows, v_rows = places(i)
-        q = side_by_side(projected[q_rows, lanes])
-        k, v = projected[k_rows, lanes], projected[v_rows, lanes]
-        scores = own_blocks(mm(k, q, 0, 0), first) * 0.125
-        expo = jnp.exp(scores - jnp.max(scores, axis=0, keepdims=True))
-        part = (expo * (1.0 / jnp.sum(expo, axis=0, keepdims=True))).astype(BF)
-        probs[i] = part
-        out = mm(v, both_blocks(part, first), 1, 0).astype(BF)
-        for r in range(4):
-            attended[pl.ds(pl.multiple_of(i // 8 * 256 + r * 64, 64), 64), lanes] = out[
-                :, r * 128 : (r + 1) * 128
-            ]
+        ids = [t * UNROLL + u for u in range(UNROLL)]
+        spots = [places(i) for i in ids]
+        queries = [side_by_side(projected[s[2], s[1]]) for s in spots]
+        keys = [projected[s[3], s[1]] for s in spots]
+        values = [projected[s[4], s[1]] for s in spots]
+        parts = []
+        for full in [mm(k, q, 0, 0) for k, q in zip(keys, queries)]:
+            scores = own_blocks(full, first) * 0.125
+            expo = jnp.exp(scores - jnp.max(scores, axis=0, keepdims=True))
+            parts.append((expo * (1.0 / jnp.sum(expo, axis=0, keepdims=True))).astype(BF))
+        outs = [mm(v, both_blocks(part, first), 1, 0).astype(BF) for v, part in zip(values, parts)]
+        for i, spot, part, out in zip(ids, spots, parts, outs):
+            probs[i] = part
+            for r in range(4):
+                rows = pl.ds(pl.multiple_of(spot[0] * 256 + r * 64, 64), 64)
+                attended[rows, spot[1]] = out[:, r * 128 : (r + 1) * 128]
 
 
 def attend_back(projected, probs, d_att, d_projected, begin, end):
-    @pl.loop(begin, end)
-    def _(i):
+    @pl.loop(begin // UNROLL, end // UNROLL)
+    def _(t):
         first = halves_mask()
-        g, lanes, q_rows, k_rows, v_rows = places(i)
-        q = side_by_side(projected[q_rows, lanes])
-        da = side_by_side(d_att[q_rows, lanes])
-        k, v = projected[k_rows, lanes], projected[v_rows, lanes]
-        part = probs[i]
-        d_probs = own_blocks(mm(v, da, 0, 0), first)
-        values = part.astype(F32)
-        inner = jnp.sum(values * d_probs, axis=0, keepdims=True)
-        d_scores = both_blocks((values * (d_probs - inner) * 0.125).astype(BF), first)
-        dq = mm(k, d_scores, 1, 0).astype(BF)
-        for r in range(4):
-            d_projected[pl.ds(pl.multiple_of(g * 256 + r * 64, 64), 64), lanes] = dq[
-                :, r * 128 : (r + 1) * 128
-            ]
-        d_projected[k_rows, lanes] = mm(q, d_scores, 1, 1).astype(BF)
-        d_projected[v_rows, lanes] = mm(da, both_blocks(part, first), 1, 1).astype(BF)
+        ids = [t * UNROLL + u for u in range(UNROLL)]
+        spots = [places(i) for i in ids]
+        queries = [side_by_side(projected[s[2], s[1]]) for s in spots]
+        outs = [side_by_side(d_att[s[2], s[1]]) for s in spots]
+        keys = [projected[s[3], s[1]] for s in spots]
+        values = [projected[s[4], s[1]] for s in spots]
+        parts = [probs[i] for i in ids]
+        d_full = [mm(v, da, 0, 0) for v, da in zip(values, outs)]
+        dv = [mm(da, both_blocks(part, first), 1, 1).astype(BF) for da, part in zip(outs, parts)]
+        d_scores = []
+        for full, part in zip(d_full, parts):
+            d_probs, wide = own_blocks(full, first), part.astype(F32)
+            inner = jnp.sum(wide * d_probs, axis=0, keepdims=True)
+            d_scores.append(both_blocks((wide * (d_probs - inner) * 0.125).astype(BF), first))
+        dq = [mm(k, ds, 1, 0).astype(BF) for k, ds in zip(keys, d_scores)]
+        dk = [mm(q, ds, 1, 1).astype(BF) for q, ds in zip(queries, d_scores)]
+        for u, spot in enumerate(spots):
+            for r in range(4):
+                rows = pl.ds(pl.multiple_of(spot[0] * 256 + r * 64, 64), 64)
+                d_projected[rows, spot[1]] = dq[u][:, r * 128 : (r + 1) * 128]
+            d_projected[spot[3], spot[1]] = dk[u]
+            d_projected[spot[4], spot[1]] = dv[u]
 
 
 def send(src, dst, sems, slot, where):
@@ -338,38 +351,62 @@
         for k, step in enumerate(SIDES):
             self.go((half, 1, step), block.at[:, self.part(step), :], self.first.at[half, k], half, 0, step)
 
-    def wide_second(self, half, step):
-        k = SIDES.index(step)
+    def rest(self, step):
+        return pl.ds(192 if step == 1 else 0, 192)
+
+    def wide_early(self, half, step):
+        k, rows = SIDES.index(step), self.rest(step)
+        src, dst = self.blocks.at[half, step % 4, :, rows, :], self.second.at[half, k, :, rows, :]
+        self.go((half, 2, step), src, dst, half, 0, step)
+
+    def wide_late(self, half, step):
+        k, rows, at = SIDES.index(step), self.part(step), step % 4
         self.copies[half, 1, step].wait_recv()
-        rows = self.part(step)
-        at = step % 4
-        mine = self.blocks[half, at, :, rows, :].astype(F32)
-        self.blocks[half, at, :, rows, :] = (mine + self.first[half, k].astype(F32)).astype(BF)
-        self.go((half, 2, step), self.blocks.at[half, at], self.second.at[half, k], half, 0, step)
-
-    def wide_last(self, half):
-        total = self.blocks[half, 0].astype(F32)
-        for k, step in enumerate(SIDES):
-            self.copies[half, 2, step].wait_recv()
-            total = total + self.second[half, k].astype(F32)
-        self.slabs[half] = total.astype(BF)
-        slab = self.slabs.at[half, (self.at(half, 1) + 2) % 4]
-        for k, step in enumerate(SIDES):
-            self.go((half, 3, step), slab.at[self.part(step), :], self.third.at[half, k], half, 1, step)
-
-    def narrow_second(self, half):
+        for b in ORDER:
+            slot = (self.at(half, 1) + b) % 4
+            mine = self.blocks[half, at, slot, rows, :].astype(F32)
+            self.blocks[half, at, slot, rows, :] = (
+                mine + self.first[half, k, slot].astype(F32)
+            ).astype(BF)
+            src, dst = self.blocks.at[half, at, slot, rows, :], self.second.at[half, k, slot, rows, :]
+            self.go((half, 2, step, b), src, dst, half, 0, step)
+
+    def wide_last(self):
+        for b in ORDER:
+            for half in range(2):
+                slot = (self.at(half, 1) + b) % 4
+                total = self.blocks[half, 0, slot].astype(F32)
+                for k, step in enumerate(SIDES):
+                    if b == 2:
+                        self.copies[half, 2, step].wait_recv()
+                    self.copies[half, 2, step, b].wait_recv()
+                    total = total + self.second[half, k, slot].astype(F32)
+                self.slabs[half, slot] = total.astype(BF)
+                slab = self.slabs.at[half, slot]
+                if b == 2:
+                    for k, step in enumerate(SIDES):
+                        src = slab.at[self.part(step), :]
+                        self.go((half, 3, step), src, self.third.at[half, k], half, 1, step)
+                elif b:
+                    k, rows = SIDES.index(b), self.rest(b)
+                    dst = self.fourth.at[half, k, rows, :]
+                    self.go((half, 4, b), slab.at[rows, :], dst, half, 1, b)
+
+    def narrow_late(self, half):
         for k, step in enumerate(SIDES):
             self.copies[half, 3, step].wait_recv()
             rows = self.part(step)
             at = (self.at(half, 1) + step) % 4
             mine = self.slabs[half, at, rows, :].astype(F32)
             self.slabs[half, at, rows, :] = (mine + self.third[half, k].astype(F32)).astype(BF)
-            self.go((half, 4, step), self.slabs.at[half, at], self.fourth.at[half, k], half, 1, step)
+            src, dst = self.slabs.at[half, at, rows, :], self.fourth.at[half, k, rows, :]
+            self.go((half, 5, step), src, dst, half, 1, step)
 
     def narrow_last(self, half):
         total = self.slabs[half, self.at(half, 1)].astype(F32)
         for k, step in enumerate(SIDES):
             self.copies[half, 4, step].wait_recv()
+            self.copies[half, 5, step].wait_recv()
             total = total + self.fourth[half, k].astype(F32)
         return total
 
@@ -455,24 +492,24 @@
     norm_rows(hidden, gain, normal, hsum)
     qkv_gather.near_sides()
     qkv_gather.near_opposite()
+    out_gather.begin()
     qkv_gather.far_sides()
-    out_gather.begin()
+    out_gather.near_sides()
     qkv_gather.across_sides()
     steps = [(0, 0), (0, 1), (0, -1), (1, 0), (-1, 0), (1, 1), (1, -1), (-1, 1)]
     early = [(x + i) % 4 * 4 + (y + j) % 4 for i, j in steps]
     every = [(i, j) for i in (0, 1, 2, -1) for j in (0, 1, 2, -1)]
     late = [(x + i) % 4 * 4 + (y + j) % 4 for i, j in every if (i, j) not in steps]
-    project_part(wt, normal, total_f, projected, early, False)
+    project_part(wt, normal, total_f, projected, early, False, 0, 4)
     qkv_gather.far_opposite()
-    out_gather.near_sides()
+    out_gather.near_opposite()
     qkv_gather.across_rest()
-    project_part(wt, normal, total_f, projected, late, True)
-    out_gather.near_opposite()
-    attend(projected, probs, attended, 0, 8)
+    project_part(wt, normal, total_f, projected, late, True, 0, 2)
     out_gather.far_sides()
-    attend(projected, probs, attended, 8, 24)
+    project_part(wt, normal, total_f, projected, late, True, 2, 4)
+    attend(projected, probs, attended, 0, 16)
     out_gather.far_opposite()
-    attend(projected, probs, attended, 24, 32)
+    attend(projected, probs, attended, 16, 32)
     out_gather.across_sides()
     out_gather.across_rest()
 
@@ -561,19 +598,21 @@
         mine = blocks[half, at].astype(F32)
         blocks[half, at] = (mine + arriving[half, at].astype(F32)).astype(BF)
 
+    def passed(step, half):
+        joined(step, half)
+        if step == 2:
+            ring.wide_first(half)
+        elif step:
+            ring.wide_early(half, step)
+
     for n, (step, half) in enumerate(units):
         unit(step, half)
         if n:
-            joined(*units[n - 1])
-            if units[n - 1][0] == 2:
-                ring.wide_first(units[n - 1][1])
-        if n == 5:
-            ring.wide_second(0, 1)
-        if n == 6:
-            ring.wide_second(1, 1)
-            ring.wide_second(0, -1)
-    joined(*units[-1])
-    ring.wide_second(1, -1)
+            passed(*units[n - 1])
+    passed(*units[-1])
+    for half in range(2):
+        for step in SIDES:
+            ring.wide_late(half, step)
 
     pair_gather.far_opposite()
     lanes = pl.ds(pl.multiple_of(D + f // 2 * 128, 128), 128)
@@ -587,10 +626,9 @@
         send(outer.at[w["z"] * 2 + w["c"]], outer_in.at[k], (list_send, list_recv), k, w)
         for k, w in enumerate(outers)
     ]
-    ring.wide_last(0)
-    ring.wide_last(1)
-    ring.narrow_second(0)
-    ring.narrow_second(1)
+    ring.wide_last()
+    ring.narrow_late(0)
+    ring.narrow_late(1)
     total = outer[z * 2 + c].astype(F32)
     for k, copy in enumerate(out_copies):
         copy.wait()
@@ -671,7 +709,7 @@
         + semaphores(10)
         + semaphores(40)
         + semaphores(8)
-        + semaphores(16)
+        + semaphores(36)
         + semaphores(10),
         compiler_params=pltpu.CompilerParams(
             vmem_limit_bytes=VMEM_CAP, has_side_effects=True, collective_id=0

time: 120 us -> 103 us (0.86)
  Pallas kernels: 114 us -> 97.6 us
    pallas_call x1, Pallas kernels: 114 us -> 97.6 us  [local(): pl.pallas_call(whole_body, out_shape=(shape(1, 1, dtype=F32), shape(128,...]
where the time goes in v3:
time: 103 us
  Pallas kernels  97.6 us (95%)
  local copies, waits for them, and re-layouts  3.12 us (3%)
  between operations  2.41 us (2%)
    pallas_call x1, Pallas kernels, local(): pl.pallas_call(whole_body, out_shape=(shape(1, 1, dtype=F32), shape(128,...  97.6 us
    unnamed x2, local copies, waits for them, and re-layouts  3.12 us

profile of v3, /device:TPU:0, one launch (start us, length us, event | category | flops | bytes accessed | tf_op | source)
XLA Modules:
  0.0 103.2 jit_solution(1476338912431901527)
XLA Ops:
  0.6 97.6 %whole.1 = (f32[1,1]{1,0:T(1,128)}, f32[128,192]{1,0:T(8,128)}, f32[64,256]{1,0:T(8,128)}) custom-call(bf16[1024,2048]{1,0:T(8,128)(2,1)} %bitcast.8, f32[1,2048]{1,0:T(1,128)} %bitcast.9, bf16[128,1536]{1,0:T(8,128)(2,1)} %w_qkv.1, bf16[64,2048]{1,0:T(8,128)(2,1)} %w_out_own.1, f32[1,2048]{1,0:T(1,128)} %bitcast.10, f32[1,2048]{1,0:T(1,128)} %bitcast.11, ...), custom_call_target="tpu_custom_call" | custom-call | tf_op jit(solution)/shard_map/whole/pallas_call | solution.py:671
  98.3 1.6 %copy.12 = f32[128,192]{0,1:T(8,128)} copy(f32[128,192]{1,0:T(8,128)} %get-tuple-element.10) | data formatting | bytes 196608
  100.6 1.5 %copy.16 = f32[64,256]{1,0:T(8,128)} copy(f32[64,256]{1,0:T(8,128)} %get-tuple-element.17) | data formatting | bytes 131072

commit v4 on v3

--- a/solution.py
+++ b/solution.py
@@ -553,7 +553,6 @@
     pair_gather.near_opposite()
     attend_back(projected, probs, d_att, d_projected, 20, 32)
     scores.wait()
-    pair_gather.far_sides()
     loss_value, factors = listwise(table, lengths, group)
     loss[...] = loss_value
     own = jnp.where(f // 8 == 0, factors[0], factors[1])
@@ -609,6 +608,8 @@
         unit(step, half)
         if n:
             passed(*units[n - 1])
+        if n == 3:
+            pair_gather.far_sides()
     passed(*units[-1])
     for half in range(2):
         for step in SIDES:
@@ -646,7 +647,7 @@
     for k, copy in enumerate(layer_copies):
         copy.wait()
         total = total + layers_in[k].astype(F32)
-    grad_qkv[...] = total.T
+    grad_qkv[...] = total
     qkv_gather.end()
     out_gather.end()
     pair_gather.end()
@@ -667,12 +668,18 @@
     return [pltpu.SemaphoreType.DMA((count,))] * 2
 
 
+def finish_body(loss, grad_qkv, grad_out, loss_to, qkv_to, out_to):
+    loss_to[...] = loss[...]
+    qkv_to[...] = grad_qkv[...].T
+    out_to[...] = grad_out[...]
+
+
 def local(hidden, norm_gain, w_qkv, w_out, final_gain, w_score, prior, labels, lengths):
     loss, grad_qkv, grad_out = pl.pallas_call(
         whole_body,
         out_shape=(
             shape(1, 1, dtype=F32),
-            shape(128, 192, dtype=F32),
+            shape(192, 128, dtype=F32),
             shape(64, 256, dtype=F32),
         ),
         in_specs=[vm()] * 9,
@@ -720,6 +727,18 @@
         final_gain.reshape(1, D), w_score.reshape(1, D),
         prior.reshape(1, PASS), labels.reshape(1, PASS), lengths.reshape(1, -1),
     )
+    loss, grad_qkv, grad_out = pl.pallas_call(
+        finish_body,
+        out_shape=(
+            shape(1, 1, dtype=F32),
+            shape(128, 192, dtype=F32),
+            shape(64, 256, dtype=F32),
+        ),
+        in_specs=[vm()] * 3,
+        out_specs=(vm(),) * 3,
+        compiler_params=pltpu.CompilerParams(vmem_limit_bytes=4 * 1024 * 1024),
+        name="finish",
+    )(loss, grad_qkv, grad_out)
     return loss.reshape(()), grad_qkv, grad_out
 
 

time: 103 us -> 102 us (level)
  between operations: 2.41 us -> 0.65 us
  Pallas kernels: 97.6 us -> 98.7 us
    pallas_call x1 -> x2, Pallas kernels: 97.6 us -> 98.7 us  [the longest x1 97.5 us: local(): pl.pallas_call(whole_body, out_shape=(shape(1, 1, dtype=F32), shape(192,...]
    unnamed x2 -> x5, local copies, waits for them, and re-layouts: 3.12 us -> 2.46 us
where the time goes in v4:
time: 102 us
  Pallas kernels  98.7 us (97%)
  local copies, waits for them, and re-layouts  2.46 us (2%)
    pallas_call x1, Pallas kernels, local(): pl.pallas_call(whole_body, out_shape=(shape(1, 1, dtype=F32), shape(192,...  97.5 us
    unnamed x5, local copies, waits for them, and re-layouts  2.46 us

profile of v4, /device:TPU:0, one launch (start us, length us, event | category | flops | bytes accessed | tf_op | source)
XLA Modules:
  0.0 101.8 jit_solution(9600342725683781408)
XLA Ops:
  0.6 97.5 %whole.1 = (f32[1,1]{1,0:T(1,128)}, f32[192,128]{1,0:T(8,128)}, f32[64,256]{1,0:T(8,128)}) custom-call(bf16[1024,2048]{1,0:T(8,128)(2,1)} %bitcast.8, f32[1,2048]{1,0:T(1,128)} %bitcast.9, bf16[128,1536]{1,0:T(8,128)(2,1)} %w_qkv.1, bf16[64,2048]{1,0:T(8,128)(2,1)} %w_out_own.1, f32[1,2048]{1,0:T(1,128)} %bitcast.10, f32[1,2048]{1,0:T(1,128)} %bitcast.11, ...), custom_call_target="tpu_custom_call" | custom-call | tf_op jit(solution)/shard_map/whole/pallas_call | solution.py:678
  98.1 0.0 copy-start
  98.1 0.9 copy-done
  99.0 0.0 copy-start.1
  99.0 0.8 copy-done.1
  99.9 1.2 %finish.1 = (f32[1,1]{1,0:T(1,128)}, f32[128,192]{1,0:T(8,128)S(1)}, f32[64,256]{1,0:T(8,128)}) custom-call(f32[1,1]{1,0:T(1,128)} %get-tuple-element.9.loss, f32[192,128]{1,0:T(8,128)S(1)} %copy-done, f32[64,256]{1,0:T(8,128)S(1)} %copy-done.1), custom_call_target="tpu_custom_call" | custom-call | tf_op jit(solution)/shard_map/finish/pallas_call | solution.py:730
  101.1 0.7 copy.12
Async XLA Ops:
  98.1 0.9 copy-start
  99.0 0.8 copy-start.1

commit v5 on v4

--- a/solution.py
+++ b/solution.py
@@ -106,8 +106,8 @@
                     self.relay((half, 4, near, step), half, 1, slot, step)
                     self.pass_on(half, near, -step)
 
-    def far_opposite(self):
-        for near in (0, 1, -1, 2):
+    def far_opposite(self, nears=(0, 1, -1, 2)):
+        for near in nears:
             for half in range(2):
                 for step in SIDES:
                     self.copies[half, 4, near, step].wait_recv()
@@ -430,9 +430,9 @@
 
 
 def whole_body(
-    hidden, gain, w_qkv, w_out_own, final_gain, w_score, prior, labels, lengths,
+    hidden_hbm, gain, w_qkv, w_out_own, final_gain, w_score, prior, labels, lengths,
     loss, grad_qkv, grad_out,
-    normal, hsum, wt, total_f, projected, probs, attended, w_blocks, table, pair,
+    hidden, hidden_sem, normal, hsum, wt, total_f, projected, probs, attended, w_blocks, table, pair,
     d_projected, everyone, wide, outer, outer_in,
     leaving, arriving, blocks, slabs, first, second, third, fourth, layers, layers_in,
     qkv_send, qkv_recv, out_send, out_recv, table_send, table_recv,
@@ -484,11 +484,14 @@
             cols = pl.ds(pl.multiple_of(core * 768 + half * 384, 128), 384)
             wt[f, qkv_rows(half, None, core), :] = w_qkv[:, cols].T
 
+    load = pltpu.make_async_copy(hidden_hbm, hidden, hidden_sem)
+    load.start()
     turned(c)
     greet(axis_peers("y", y) + axis_peers("x", x) + outers)
     qkv_gather.begin()
     turned(1 - c)
     w_blocks[f] = w_out_own[...]
+    load.wait()
     norm_rows(hidden, gain, normal, hsum)
     qkv_gather.near_sides()
     qkv_gather.near_opposite()
@@ -682,9 +685,11 @@
             shape(192, 128, dtype=F32),
             shape(64, 256, dtype=F32),
         ),
-        in_specs=[vm()] * 9,
+        in_specs=[pl.BlockSpec(memory_space=pl.ANY)] + [vm()] * 8,
         out_specs=(vm(),) * 3,
         scratch_shapes=[
+            pltpu.VMEM((ROWS, D), BF),
+            pltpu.SemaphoreType.DMA,
             pltpu.VMEM((ROWS, D), BF),
             pltpu.VMEM((PASS, D), F32),
             pltpu.VMEM((16, COLS, 128), BF),

time: 102 us -> 101 us (level)
  Pallas kernels: 98.7 us -> 97.4 us
    pallas_call x1, Pallas kernels: 97.5 us -> 96.2 us  [local(): pl.pallas_call(whole_body, out_shape=(shape(1, 1, dtype=F32), shape(192,...]
where the time goes in v5:
time: 101 us
  Pallas kernels  97.4 us (96%)
  local copies, waits for them, and re-layouts  2.46 us (2%)
    pallas_call x1, Pallas kernels, local(): pl.pallas_call(whole_body, out_shape=(shape(1, 1, dtype=F32), shape(192,...  96.2 us
    unnamed x5, local copies, waits for them, and re-layouts  2.46 us

profile of v5, /device:TPU:0, one launch (start us, length us, event | category | flops | bytes accessed | tf_op | source)
XLA Modules:
  0.0 100.5 jit_solution(7605619762484140357)
XLA Ops:
  0.6 96.2 %whole.1 = (f32[1,1]{1,0:T(1,128)}, f32[192,128]{1,0:T(8,128)}, f32[64,256]{1,0:T(8,128)}) custom-call(bf16[1024,2048]{1,0:T(8,128)(2,1)} %bitcast.8, f32[1,2048]{1,0:T(1,128)} %bitcast.9, bf16[128,1536]{1,0:T(8,128)(2,1)} %w_qkv.1, bf16[64,2048]{1,0:T(8,128)(2,1)} %w_out_own.1, f32[1,2048]{1,0:T(1,128)} %bitcast.10, f32[1,2048]{1,0:T(1,128)} %bitcast.11, ...), custom_call_target="tpu_custom_call" | custom-call | tf_op jit(solution)/shard_map/whole/pallas_call | solution.py:681
  96.9 0.0 copy-start
  96.9 0.9 copy-done
  97.8 0.0 copy-start.1
  97.8 0.8 copy-done.1
  98.6 1.2 %finish.1 = (f32[1,1]{1,0:T(1,128)}, f32[128,192]{1,0:T(8,128)S(1)}, f32[64,256]{1,0:T(8,128)}) custom-call(f32[1,1]{1,0:T(1,128)} %get-tuple-element.9.loss, f32[192,128]{1,0:T(8,128)S(1)} %copy-done, f32[64,256]{1,0:T(8,128)S(1)} %copy-done.1), custom_call_target="tpu_custom_call" | custom-call | tf_op jit(solution)/shard_map/finish/pallas_call | solution.py:735
  99.8 0.7 copy.12
Async XLA Ops:
  96.9 0.9 copy-start
  97.8 0.8 copy-start.1
